TPU v7x, 1024 devices: a whole 4x8x16 slice. The times are simulated.
1024 devices in a mesh: sect: 16 (over z), tx: 16 (over x_hi, y), ty: 4 (over x_lo, core).
Axes of the slice: x: 4 (x_hi: 2, x_lo: 2; x = x_hi * 2 + x_lo), y: 8, z: 16, core: 2. Of those that a mesh axis runs over, the one named last changes fastest.
Arguments:
- solute_amounts: float32 [19, 16, 32, 8192], P(None, None, 'sect', ('tx', 'ty')), may hold values from 0.2 to 2
- submerged_layer_tally: int32 [32, 8192], P('sect', ('tx', 'ty')), may hold values from 0 to 16
- zonal_boundary_transport: float32 [16, 32, 8192], P('sect', None, ('tx', 'ty')), may hold values from -0.25 to 0.25
- meridional_boundary_transport: float32 [16, 32, 8192], P('sect', None, ('tx', 'ty')), may hold values from -0.25 to 0.25
- diffusion_factor: float32 [16, 32, 8192], P('sect', None, ('tx', 'ty')), may hold values from 0.05 to 5
- thermal_state: float32 [16, 32, 8192], P('sect', None, ('tx', 'ty')), may hold values from -2 to 30
- saltiness_field: float32 [16, 32, 8192], P('sect', None, ('tx', 'ty')), may hold values from 32 to 38
- chemistry_matrix: float32 [19, 19], replicated, may hold values from -1.25 to 1.25
Outputs:
- advanced_solutes: float32 [19, 16, 32, 8192], P(None, None, 'sect', ('tx', 'ty'))
- heating: float32 [16, 32, 8192], P('sect', None, ('tx', 'ty'))
All inputs are finite; a program needn't handle non-finite values.
Results may differ from a plain program's by a relative error of at most 0.0003.
Values sent between devices are 32-bit elements; how exact they have to be, the bound alone decides.
No kernel may reach another device: no remote copies, remote signals or barrier semaphores. Data moves between devices by JAX's collectives and lax.ppermute only.
A program may use at most 32 MiB of HBM per device.

v0:
```python
import jax
import jax.numpy as jnp
from jax import lax
from jax.sharding import PartitionSpec as P


def with_halo(block, sides, width):
    for axis, dim in sides:
        count = lax.axis_size(axis)
        forward = [(i, i + 1) for i in range(count - 1)]
        backward = [(target, source) for source, target in forward]
        low = lax.ppermute(
            lax.slice_in_dim(block, block.shape[dim] - width, None, axis=dim), axis, forward
        )
        high = lax.ppermute(lax.slice_in_dim(block, 0, width, axis=dim), axis, backward)
        block = jnp.concatenate([low, block, high], axis=dim)
    return block


def prefix(array, axis, combine, identity):
    devices, position = (lax.axis_size(axis), lax.axis_index(axis))
    everything = lax.all_gather(array, axis)
    start = jnp.broadcast_to(jnp.asarray(identity, array.dtype), array.shape)

    def step(k, before):
        reached = k < position
        new = combine(before, everything[k])
        return jnp.where(reached, new, before)

    return lax.fori_loop(0, devices, step, start)


def window(array, start, length, along):
    return lax.slice_in_dim(array, start, start + length, axis=along)


def minmod(first, second):
    return jnp.where(
        first * second > 0, jnp.sign(first) * jnp.minimum(jnp.abs(first), jnp.abs(second)), 0.0
    )


def sweep(values, courant, along, length):
    far_low = window(values, 0, length + 1, along)
    near_low = window(values, 1, length + 1, along)
    near_high = window(values, 2, length + 1, along)
    far_high = window(values, 3, length + 1, along)
    upwind_east = near_low + 0.5 * (1.0 - courant) * minmod(
        near_low - far_low, near_high - near_low
    )
    upwind_west = near_high - 0.5 * (1.0 + courant) * minmod(
        near_high - near_low, far_high - near_high
    )
    face_flux = courant * jnp.where(courant >= 0, upwind_east, upwind_west)
    return window(face_flux, 0, length, along) - window(face_flux, 1, length, along)


def advect(conc_pad, wet_pad, east_faces, north_faces):
    cells_x = conc_pad.shape[2] - 4
    cells_y = conc_pad.shape[3] - 4
    inner_y = conc_pad[:, :, :, 2 : cells_y + 2]
    mask_y = wet_pad[:, :, 2 : cells_y + 2]
    open_x = mask_y[:, 1 : cells_x + 2] * mask_y[:, 2 : cells_x + 3]
    tend_x = sweep(inner_y, east_faces * open_x, 2, cells_x)
    inner_x = conc_pad[:, :, 2 : cells_x + 2, :]
    mask_x = wet_pad[:, 2 : cells_x + 2, :]
    open_y = mask_x[:, :, 1 : cells_y + 2] * mask_x[:, :, 2 : cells_y + 3]
    tend_y = sweep(inner_x, north_faces * open_y, 3, cells_y)
    return conc_pad[:, :, 2 : cells_x + 2, 2 : cells_y + 2] + tend_x + tend_y


def diffuse(moved, diffusion_factor, ocean_indicator):
    lower_mask = jnp.concatenate([ocean_indicator[1:], jnp.zeros_like(ocean_indicator[:1])], 0)
    coupling = diffusion_factor * ocean_indicator * lower_mask
    upper_link = jnp.concatenate([jnp.zeros_like(coupling[:1]), coupling[:-1]], 0)
    diagonal = 1.0 + upper_link + coupling
    source_all = jnp.moveaxis(moved, 1, 0)

    def forward(carry, inputs):
        sweep_ratio, sweep_rhs = carry
        diag_now, upper_now, coupling_now, source = inputs
        divisor = diag_now + upper_now * sweep_ratio
        new_ratio = -coupling_now / divisor
        new_rhs = (source + upper_now[None] * sweep_rhs) / divisor[None]
        return ((new_ratio, new_rhs), (new_ratio, new_rhs))

    start = (
        jnp.zeros(diagonal.shape[1:], jnp.float32),
        jnp.zeros(source_all.shape[1:], jnp.float32),
    )
    unused, (ratios, rhs_all) = lax.scan(
        forward, start, (diagonal, upper_link, coupling, source_all)
    )

    def backward(following, inputs):
        sweep_ratio, sweep_rhs = inputs
        solved = sweep_rhs - sweep_ratio[None] * following
        return (solved, solved)

    unused, solved_all = lax.scan(
        backward, jnp.zeros(source_all.shape[1:], jnp.float32), (ratios, rhs_all), reverse=True
    )
    return jnp.moveaxis(solved_all, 0, 1)


def perform_chemistry(
    blended_solutes, thermal_state, saltiness_field, chemistry_matrix, ocean_indicator
):
    expansion_speed = jnp.exp(0.0633 * (thermal_state - 15.0)) * (
        1.0 + 0.25 * (saltiness_field - 35.0)
    )
    reacted = jnp.einsum(
        "ij,jkxy->ikxy", chemistry_matrix, blended_solutes, precision=lax.Precision.HIGHEST
    )
    return ocean_indicator[None] * (blended_solutes + 0.2 * expansion_speed[None] * reacted)


def add_depth(earlier, later):
    return earlier + later


def body(
    solute_amounts,
    submerged_layer_tally,
    zonal_boundary_transport,
    meridional_boundary_transport,
    diffusion_factor,
    thermal_state,
    saltiness_field,
    chemistry_matrix,
):
    tracer_count = solute_amounts.shape[0]
    cells_x = solute_amounts.shape[2]
    cells_y = solute_amounts.shape[3]
    east, north, kappa, temp_here, salt_here = (
        lax.all_to_all(zonal_boundary_transport, "sect", split_axis=1, concat_axis=0, tiled=True),
        lax.all_to_all(
            meridional_boundary_transport, "sect", split_axis=1, concat_axis=0, tiled=True
        ),
        lax.all_to_all(diffusion_factor, "sect", split_axis=1, concat_axis=0, tiled=True),
        lax.all_to_all(thermal_state, "sect", split_axis=1, concat_axis=0, tiled=True),
        lax.all_to_all(saltiness_field, "sect", split_axis=1, concat_axis=0, tiled=True),
    )
    depth_index = lax.broadcasted_iota(jnp.int32, east.shape, 0)
    ocean_indicator = (depth_index < submerged_layer_tally[None]).astype(jnp.float32)
    tracer_now = solute_amounts * ocean_indicator[None]
    stacked = jnp.concatenate([tracer_now, ocean_indicator[None], east[None], north[None]], 0)
    padded = with_halo(stacked, (("sect", 2), (("tx", "ty"), 3)), 2)
    conc_pad = padded[:tracer_count]
    wet_pad = padded[tracer_count]
    east_faces = padded[tracer_count + 1][:, 1 : cells_x + 2, 2 : cells_y + 2]
    north_faces = padded[tracer_count + 2][:, 2 : cells_x + 2, 1 : cells_y + 2]
    moved = advect(conc_pad, wet_pad, east_faces, north_faces)
    blended_solutes = diffuse(moved, kappa, ocean_indicator)
    advanced_solutes = perform_chemistry(
        blended_solutes, temp_here, salt_here, chemistry_matrix, ocean_indicator
    )
    absorption = ocean_indicator * (0.02 + 0.04 * jnp.maximum(advanced_solutes[0], 0.0))
    ocean_absorb = lax.all_to_all(absorption, "sect", split_axis=0, concat_axis=1, tiled=True)
    local_total = jnp.sum(ocean_absorb, 0)
    above_total = prefix(local_total, "sect", add_depth, jnp.zeros_like(local_total))
    optical_depth = above_total[None] + jnp.cumsum(ocean_absorb, 0) - ocean_absorb
    heating = 16.0 * jnp.exp(-optical_depth) * (1.0 - jnp.exp(-ocean_absorb))
    return (advanced_solutes, heating)


def solution(mesh):
    in_specs = (
        P(None, None, "sect", ("tx", "ty")),
        P("sect", ("tx", "ty")),
        P("sect", None, ("tx", "ty")),
        P("sect", None, ("tx", "ty")),
        P("sect", None, ("tx", "ty")),
        P("sect", None, ("tx", "ty")),
        P("sect", None, ("tx", "ty")),
        P(),
    )
    out_specs = (P(None, None, "sect", ("tx", "ty")), P("sect", None, ("tx", "ty")))
    return jax.shard_map(body, mesh=mesh, in_specs=in_specs, out_specs=out_specs, check_vma=False)
```

profile of v0, /device:TPU:32, one launch (start us, length us, event | category | flops | bytes accessed | tf_op | source)
XLA Modules:
  0.0 181.0 jit_solution(4300741465257146907)
XLA Ops:
  0.7 18.9 %all-to-all-start.1 = ((f32[1,32,128]{2,0,1:T(1,128)}), f32[1,32,128]{2,0,1:T(1,128)S(1)}, u32[]{:S(2)}, u32[]{:S(2)}) async-start(f32[1,32,128]{2,0,1:T(1,128)} %bitcast.98), calls=%async_computation.1 | async-start | bytes 32768 | tf_op jit(solution)/shard_map/all_to_all | solution.py:136
  20.2 1.2 copy_multiply_fusion
  21.4 10.7 %all-to-all-done.1 = f32[1,32,128]{2,0,1:T(1,128)S(1)} async-done(((f32[1,32,128]{2,0,1:T(1,128)}), f32[1,32,128]{2,0,1:T(1,128)S(1)}, u32[]{:S(2)}, u32[]{:S(2)}) %all-to-all-start.1) | async-done | bytes 16416 | tf_op jit(solution)/shard_map/all_to_all | solution.py:136
  32.1 3.5 %all-to-all-start.2 = ((f32[1,32,128]{2,0,1:T(1,128)}), f32[1,32,128]{2,0,1:T(1,128)S(1)}, u32[]{:S(2)}, u32[]{:S(2)}) async-start(f32[1,32,128]{2,0,1:T(1,128)} %bitcast.99), calls=%async_computation.2 | async-start | bytes 32768 | tf_op jit(solution)/shard_map/all_to_all | solution.py:137
  36.3 11.6 %all-to-all-done.2 = f32[1,32,128]{2,0,1:T(1,128)S(1)} async-done(((f32[1,32,128]{2,0,1:T(1,128)}), f32[1,32,128]{2,0,1:T(1,128)S(1)}, u32[]{:S(2)}, u32[]{:S(2)}) %all-to-all-start.2) | async-done | bytes 16416 | tf_op jit(solution)/shard_map/all_to_all | solution.py:137
  47.9 3.5 %all-to-all-start = ((f32[1,32,128]{2,0,1:T(1,128)}), f32[1,32,128]{2,0,1:T(1,128)S(1)}, u32[]{:S(2)}, u32[]{:S(2)}) async-start(f32[1,32,128]{2,0,1:T(1,128)} %bitcast.100), calls=%async_computation | async-start | bytes 32768 | tf_op jit(solution)/shard_map/all_to_all | solution.py:140
  51.5 3.7 %collective-permute-start = (f32[22,16,2,128]{3,0,2,1:T(8,128)S(1)}, f32[22,16,2,128]{3,0,2,1:T(8,128)S(1)}, u32[]{:S(2)}, u32[]{:S(2)}) collective-permute-start(f32[22,16,2,128]{3,0,2,1:T(8,128)S(1)} %pad_maximum_fusion.17), channel_id=1, source_target_pairs={{0,64},{64,128},{128,192},{192,256},{256,320},{320,384},{384,448},... | collective-permute-start | bytes 1081352 | tf_op jit(solution)/shard_map/ppermute | solution.py:12
  55.3 1.3 collective-permute-start.1
  56.6 7.5 %all-to-all-done = f32[1,32,128]{2,0,1:T(1,128)S(1)} async-done(((f32[1,32,128]{2,0,1:T(1,128)}), f32[1,32,128]{2,0,1:T(1,128)S(1)}, u32[]{:S(2)}, u32[]{:S(2)}) %all-to-all-start) | async-done | bytes 16416 | tf_op jit(solution)/shard_map/all_to_all | solution.py:140
  64.1 6.5 %all-to-all-start.3 = ((f32[1,32,128]{2,0,1:T(1,128)}), f32[1,32,128]{2,0,1:T(1,128)S(1)}, u32[]{:S(2)}, u32[]{:S(2)}) async-start(f32[1,32,128]{2,0,1:T(1,128)} %bitcast.11), calls=%async_computation.3 | async-start | bytes 32768 | tf_op jit(solution)/shard_map/all_to_all | solution.py:141
  70.6 12.5 %all-to-all-done.3 = f32[1,32,128]{2,0,1:T(1,128)S(1)} async-done(((f32[1,32,128]{2,0,1:T(1,128)}), f32[1,32,128]{2,0,1:T(1,128)S(1)}, u32[]{:S(2)}, u32[]{:S(2)}) %all-to-all-start.3) | async-done | bytes 16416 | tf_op jit(solution)/shard_map/all_to_all | solution.py:141
  83.1 3.5 %all-to-all-start.4 = ((f32[1,32,128]{2,0,1:T(1,128)}), f32[1,32,128]{2,0,1:T(1,128)S(1)}, u32[]{:S(2)}, u32[]{:S(2)}) async-start(f32[1,32,128]{2,0,1:T(1,128)} %bitcast.13), calls=%async_computation.4 | async-start | bytes 32768 | tf_op jit(solution)/shard_map/all_to_all | solution.py:142
  87.2 11.7 %all-to-all-done.4 = f32[1,32,128]{2,0,1:T(1,128)S(1)} async-done(((f32[1,32,128]{2,0,1:T(1,128)}), f32[1,32,128]{2,0,1:T(1,128)S(1)}, u32[]{:S(2)}, u32[]{:S(2)}) %all-to-all-start.4) | async-done | bytes 16416 | tf_op jit(solution)/shard_map/all_to_all | solution.py:142
  100.1 1.3 copy.80
  101.4 2.0 %collective-permute-start.2 = (f32[22,16,6,2]{0,1,3,2:T(8,128)}, f32[22,16,6,2]{0,1,3,2:T(8,128)S(1)}, u32[]{:S(2)}, u32[]{:S(2)}) collective-permute-start(f32[22,16,6,2]{0,1,3,2:T(8,128)} %copy.80), channel_id=1, source_target_pairs={{0,1},{1,2},{2,3},{3,4},{4,5},{5,6},{6,7},{7,8},{8,9},{9,10},{10,1... | collective-permute-start | bytes 50696 | tf_op jit(solution)/shard_map/ppermute | solution.py:12
  104.2 5.7 %collective-permute-start.3 = (f32[22,16,6,2]{0,1,3,2:T(8,128)S(1)}, f32[22,16,6,2]{0,1,3,2:T(8,128)}, u32[]{:S(2)}, u32[]{:S(2)}) collective-permute-start(f32[22,16,6,2]{0,1,3,2:T(8,128)S(1)} %copy.81), channel_id=1, source_target_pairs={{1,0},{2,1},{3,2},{4,3},{5,4},{6,5},{7,6},{8,7},{9,8},{10,9},{11,1... | collective-permute-start | bytes 50696 | tf_op jit(solution)/shard_map/ppermute | solution.py:15
  109.9 1.4 maximum_maximum_fusion
  112.1 1.6 copy.83
  113.7 1.9 %pad_maximum_fusion = f32[22,16,6,132]{3,0,2,1:T(8,128)S(1)} fusion(f32[22,16,6,2]{3,0,2,1:T(8,128)S(1)} %copy.83, f32[22,16,2,128]{3,0,2,1:T(8,128)S(1)} %collective-permute-done.1, f32[1,16,2,128]{3,0,2,1:T(1,128)} %bitcast.87, f32[1,16,2,128]{3,0,2,1:T(1,128)} %bitcast.82, f32[1,16,2,128]{3,0,2,1:T(1,128)} %copy-done.10, ...), kind=kLoop, calls=%fused_computation.20 | loop fusion | flops 1951488 | bytes 2230272 | tf_op jit(solution)/shard_map/concatenate | solution.py:16
  117.8 2.6 %select_multiply_fusion.3 = f32[19,16,2,129]{3,0,2,1:T(8,128)S(1)} fusion(f32[22,16,6,2]{3,0,2,1:T(8,128)S(1)} %copy.83, f32[22,16,2,128]{3,0,2,1:T(8,128)S(1)} %collective-permute-done.1, f32[1,16,2,128]{3,0,2,1:T(1,128)S(1)} %bitcast.89, f32[1,16,2,128]{3,0,2,1:T(1,128)S(1)} %bitcast.84, f32[1,16,2,128]{3,0,2,1:T(1,128)S(1)} %copy-done.12, ...), kind=kLoop, calls=%fused_computation.44 | loop fusion | flops 3764736 | bytes 1482528 | tf_op jit(solution)/shard_map/mul | solution.py:54
  121.1 12.2 %while.48 = (s32[]{:T(128)}, f32[2,128]{1,0:T(2,128)S(1)}, f32[19,2,128]{2,1,0:T(2,128)S(1)}, f32[16,2,128]{2,1,0:T(2,128)S(1)}, f32[16,19,2,128]{3,2,1,0:T(2,12...) while((s32[]{:T(128)}, f32[2,128]{1,0:T(2,128)S(1)}, ...), condition=%wide.region_1.2_spmd.clone, body=%wide.region_0.1_spmd.clone.sunk | while | flops 20739 | bytes 88192 | solution.py:91
  135.7 3.5 %all-to-all-start.5 = ((f32[16,2,128]{2,1,0:T(2,128)}), f32[16,2,128]{2,1,0:T(2,128)S(1)}, u32[]{:S(2)}, u32[]{:S(2)}) async-start(f32[16,2,128]{2,1,0:T(2,128)} %fusion.28), calls=%async_computation.5 | async-start | bytes 32768 | tf_op jit(solution)/shard_map/all_to_all | solution.py:159
  140.1 11.5 %all-to-all-done.5 = f32[16,2,128]{2,1,0:T(2,128)S(1)} async-done(((f32[16,2,128]{2,1,0:T(2,128)}), f32[16,2,128]{2,1,0:T(2,128)S(1)}, u32[]{:S(2)}, u32[]{:S(2)}) %all-to-all-start.5) | async-done | bytes 16416 | tf_op jit(solution)/shard_map/all_to_all | solution.py:159
  151.6 28.2 %all_gather.4 = f32[16,32,128]{2,1,0:T(8,128)S(1)} all-gather(f32[1,32,128]{2,1,0:T(8,128)S(1)} %bitcast.91), channel_id=1, replica_groups=mesh['sect'=16,'tx'=16,'ty'=4] {'sect'}, dimensions={0}, use_global_device_ids=true | all-gather | bytes 278528 | tf_op jit(solution)/shard_map/all_gather | solution.py:22
  (172 shorter events, 24.4 us)
Async XLA Ops:
  0.6 133.9 %copy-start = (f32[19,19]{1,0:T(8,128)S(1)}, f32[19,19]{1,0:T(8,128)}, u32[]{:S(2)}) copy-start(f32[19,19]{1,0:T(8,128)} %param.21) | copy-start | bytes 4336
  0.6 69.9 %copy-start.20 = (s32[2,128]{1,0:T(2,128)S(1)}, s32[2,128]{1,0:T(2,128)}, u32[]{:S(2)}) copy-start(s32[2,128]{1,0:T(2,128)} %param.15) | copy-start | bytes 3076
  0.7 31.4 %all-to-all-start.1 = ((f32[1,32,128]{2,0,1:T(1,128)}), f32[1,32,128]{2,0,1:T(1,128)S(1)}, u32[]{:S(2)}, u32[]{:S(2)}) async-start(f32[1,32,128]{2,0,1:T(1,128)} %bitcast.98), calls=%async_computation.1 | async-start | bytes 32768 | tf_op jit(solution)/shard_map/all_to_all | solution.py:136
  20.2 31.2 %copy-start.15 = (f32[16,2,128]{2,1,0:T(2,128)}, f32[16,2,128]{2,1,0:T(2,128)S(1)}, u32[]{:S(2)}) copy-start(f32[16,2,128]{2,1,0:T(2,128)S(1)} %fusion.29) | copy-start | bytes 49156
  32.1 67.5 %copy-start.4 = (f32[1,32,128]{2,0,1:T(1,128)}, f32[1,32,128]{2,0,1:T(1,128)S(1)}, u32[]{:S(2)}) copy-start(f32[1,32,128]{2,0,1:T(1,128)S(1)} %all-to-all-done.1) | copy-start | bytes 49156
  32.1 15.9 %all-to-all-start.2 = ((f32[1,32,128]{2,0,1:T(1,128)}), f32[1,32,128]{2,0,1:T(1,128)S(1)}, u32[]{:S(2)}, u32[]{:S(2)}) async-start(f32[1,32,128]{2,0,1:T(1,128)} %bitcast.99), calls=%async_computation.2 | async-start | bytes 32768 | tf_op jit(solution)/shard_map/all_to_all | solution.py:137
  36.3 63.3 %copy-start.10 = (f32[1,16,2,128]{3,0,2,1:T(1,128)}, f32[1,16,2,128]{3,0,2,1:T(1,128)S(1)}, u32[]{:S(2)}) copy-start(f32[1,16,2,128]{3,0,2,1:T(1,128)S(1)} %compare_convert_fusion) | copy-start | bytes 49156
  47.9 51.7 %copy-start.7 = (f32[1,32,128]{2,0,1:T(1,128)}, f32[1,32,128]{2,0,1:T(1,128)S(1)}, u32[]{:S(2)}) copy-start(f32[1,32,128]{2,0,1:T(1,128)S(1)} %all-to-all-done.2) | copy-start | bytes 49156
  47.9 16.2 %all-to-all-start = ((f32[1,32,128]{2,0,1:T(1,128)}), f32[1,32,128]{2,0,1:T(1,128)S(1)}, u32[]{:S(2)}, u32[]{:S(2)}) async-start(f32[1,32,128]{2,0,1:T(1,128)} %bitcast.100), calls=%async_computation | async-start | bytes 32768 | tf_op jit(solution)/shard_map/all_to_all | solution.py:140
  51.5 48.1 %collective-permute-start = (f32[22,16,2,128]{3,0,2,1:T(8,128)S(1)}, f32[22,16,2,128]{3,0,2,1:T(8,128)S(1)}, u32[]{:S(2)}, u32[]{:S(2)}) collective-permute-start(f32[22,16,2,128]{3,0,2,1:T(8,128)S(1)} %pad_maximum_fusion.17), channel_id=1, source_target_pairs={{0,64},{64,128},{128,192},{192,256},{256,320},{320,384},{384,448},... | collective-permute-start | bytes 1081352 | tf_op jit(solution)/shard_map/ppermute | solution.py:12
  55.3 44.3 %collective-permute-start.1 = (f32[22,16,2,128]{3,0,2,1:T(8,128)S(1)}, f32[22,16,2,128]{3,0,2,1:T(8,128)S(1)}, u32[]{:S(2)}, u32[]{:S(2)}) collective-permute-start(f32[22,16,2,128]{3,0,2,1:T(8,128)S(1)} %pad_maximum_fusion.17), channel_id=1, source_target_pairs={{64,0},{128,64},{192,128},{256,192},{320,256},{384,320},{448,384},... | collective-permute-start | bytes 1081352 | tf_op jit(solution)/shard_map/ppermute | solution.py:15
  64.1 19.0 %all-to-all-start.3 = ((f32[1,32,128]{2,0,1:T(1,128)}), f32[1,32,128]{2,0,1:T(1,128)S(1)}, u32[]{:S(2)}, u32[]{:S(2)}) async-start(f32[1,32,128]{2,0,1:T(1,128)} %bitcast.11), calls=%async_computation.3 | async-start | bytes 32768 | tf_op jit(solution)/shard_map/all_to_all | solution.py:141
  70.6 29.0 %copy-start.18 = (f32[16,2,128]{2,1,0:T(2,128)}, f32[16,2,128]{2,1,0:T(2,128)S(1)}, u32[]{:S(2)}) copy-start(f32[16,2,128]{2,1,0:T(2,128)S(1)} %pad_multiply_fusion) | copy-start | bytes 49156
  83.1 15.9 %all-to-all-start.4 = ((f32[1,32,128]{2,0,1:T(1,128)}), f32[1,32,128]{2,0,1:T(1,128)S(1)}, u32[]{:S(2)}, u32[]{:S(2)}) async-start(f32[1,32,128]{2,0,1:T(1,128)} %bitcast.13), calls=%async_computation.4 | async-start | bytes 32768 | tf_op jit(solution)/shard_map/all_to_all | solution.py:142
  101.4 8.5 %copy-start.5 = (f32[1,32,128]{2,0,1:T(1,128)S(1)}, f32[1,32,128]{2,0,1:T(1,128)}, u32[]{:S(2)}) copy-start(f32[1,32,128]{2,0,1:T(1,128)} %copy-done.4) | copy-start | bytes 49156
  101.4 8.5 %copy-start.8 = (f32[1,32,128]{2,0,1:T(1,128)S(1)}, f32[1,32,128]{2,0,1:T(1,128)}, u32[]{:S(2)}) copy-start(f32[1,32,128]{2,0,1:T(1,128)} %copy-done.7) | copy-start | bytes 49156
  101.4 8.5 %copy-start.11 = (f32[1,16,2,128]{3,0,2,1:T(1,128)S(1)}, f32[1,16,2,128]{3,0,2,1:T(1,128)}, u32[]{:S(2)}) copy-start(f32[1,16,2,128]{3,0,2,1:T(1,128)} %copy-done.10) | copy-start | bytes 49156
  101.4 9.9 %collective-permute-start.2 = (f32[22,16,6,2]{0,1,3,2:T(8,128)}, f32[22,16,6,2]{0,1,3,2:T(8,128)S(1)}, u32[]{:S(2)}, u32[]{:S(2)}) collective-permute-start(f32[22,16,6,2]{0,1,3,2:T(8,128)} %copy.80), channel_id=1, source_target_pairs={{0,1},{1,2},{2,3},{3,4},{4,5},{5,6},{6,7},{7,8},{8,9},{9,10},{10,1... | collective-permute-start | bytes 50696 | tf_op jit(solution)/shard_map/ppermute | solution.py:12
  104.2 7.9 %collective-permute-start.3 = (f32[22,16,6,2]{0,1,3,2:T(8,128)S(1)}, f32[22,16,6,2]{0,1,3,2:T(8,128)}, u32[]{:S(2)}, u32[]{:S(2)}) collective-permute-start(f32[22,16,6,2]{0,1,3,2:T(8,128)S(1)} %copy.81), channel_id=1, source_target_pairs={{1,0},{2,1},{3,2},{4,3},{5,4},{6,5},{7,6},{8,7},{9,8},{10,9},{11,1... | collective-permute-start | bytes 50696 | tf_op jit(solution)/shard_map/ppermute | solution.py:15
  120.7 12.7 %copy-start.13 = (f32[19,2,128]{2,1,0:T(2,128)S(1)}, f32[19,2,128]{2,1,0:T(2,128)}, u32[]{:S(2)}) copy-start(f32[19,2,128]{2,1,0:T(2,128)} %custom-call.2) | copy-start | bytes 58372
  120.7 13.9 %copy-start.17 = (f32[16,2,128]{2,1,0:T(2,128)S(1)}, f32[16,2,128]{2,1,0:T(2,128)}, u32[]{:S(2)}) copy-start(f32[16,2,128]{2,1,0:T(2,128)} %copy-done.15) | copy-start | bytes 49156
  120.7 13.9 %copy-start.19 = (f32[1,32,128]{2,1,0:T(8,128)S(1)}, f32[1,32,128]{2,1,0:T(8,128)}, u32[]{:S(2)}) copy-start(f32[1,32,128]{2,1,0:T(8,128)} %multiply_multiply_fusion) | copy-start | bytes 49156
  121.1 14.0 %copy-start.21 = (s32[2,128]{1,0:T(2,128)S(1)}, s32[2,128]{1,0:T(2,128)}, u32[]{:S(2)}) copy-start(s32[2,128]{1,0:T(2,128)} %param.15) | copy-start | bytes 3076
  135.7 15.9 %all-to-all-start.5 = ((f32[16,2,128]{2,1,0:T(2,128)}), f32[16,2,128]{2,1,0:T(2,128)S(1)}, u32[]{:S(2)}, u32[]{:S(2)}) async-start(f32[16,2,128]{2,1,0:T(2,128)} %fusion.28), calls=%async_computation.5 | async-start | bytes 32768 | tf_op jit(solution)/shard_map/all_to_all | solution.py:159
  (8 other events, 10.7 us)
where the time goes:
time: 182 us; the launch traced here: 181 us
  waiting for transfers between devices  65.7 us (36%)
  starting transfers between devices  52.1 us (29%)
  blocking collectives  28.2 us (15%)
  other arithmetic  24.9 us (14%)
  local copies, waits for them, and re-layouts  7.24 us (4%)
    all_gather x1, blocking collectives, prefix(): everything = lax.all_gather(array, axis)  28.2 us
    all_to_all x1, starting transfers between devices, body(): lax.all_to_all(zonal_boundary_transport, 'sect', split_axis=1, concat_axi...  18.9 us
    all_to_all x1, waiting for transfers between devices, body(): lax.all_to_all(thermal_state, 'sect', split_axis=1, concat_axis=0, tiled=...  12.5 us
    dynamic_update_slice x48, other arithmetic, diffuse(): lax.scan(forward, start, (diagonal, upper_link, coupling, source_all))  12.4 us
    all_to_all x1, waiting for transfers between devices, body(): lax.all_to_all(saltiness_field, 'sect', split_axis=1, concat_axis=0, tile...  11.7 us
    all_to_all x1, waiting for transfers between devices, body(): lax.all_to_all(meridional_boundary_transport, 'sect', split_axis=1, conca...  11.6 us
    all_to_all x1, waiting for transfers between devices, body(): lax.all_to_all(absorption, 'sect', split_axis=0, concat_axis=1, tiled=True)  11.5 us
    all_to_all x1, waiting for transfers between devices, body(): lax.all_to_all(zonal_boundary_transport, 'sect', split_axis=1, concat_axi...  10.7 us
  transfers between devices with their start and end apart: 10, of which 7 were waited for; matrix products, arithmetic and copies ran while one was open for 4% of the time, Pallas kernels for 0%

commit v1 on v0

v1 whole, which is shorter than its diff:
```python
import jax
import jax.numpy as jnp
from jax import lax
from jax.experimental import pallas as pl
from jax.experimental.pallas import tpu as pltpu
from jax.sharding import PartitionSpec as P

NTR = 19
LEV = 16
LANES = 128
BLOCK = 2 * LEV
ROWS = 12
EAST_LOW, EAST, NORTH, EDGE_LOW, EDGE_HIGH, KAPPA, GROWTH = 0, 1, 3, 5, 6, 7, 9


def lane_index():
    return lax.broadcasted_iota(jnp.int32, (LEV, LANES), 1)


def row_index():
    return lax.broadcasted_iota(jnp.int32, (LEV, LANES), 0)


def rows(ref, start, stride):
    return ref[pl.ds(start, LEV, stride=stride), :]


def minmod(first, second):
    return jnp.maximum(jnp.minimum(first, second), 0.0) + jnp.minimum(
        jnp.maximum(first, second), 0.0
    )


def pack_fields(east, north, kappa, temp, salt, north_left, out):
    def put(place, value):
        out[pl.ds(place, LEV, stride=ROWS), :] = value

    put(ROWS - 1, jnp.zeros((LEV, LANES), jnp.float32))
    low_half = lane_index() < LANES // 2
    even, odd = (rows(east, 0, 2), rows(east, 1, 2))
    put(EAST_LOW, jnp.where(row_index() == 0, 0.0, pltpu.roll(odd, 1, 0)))
    put(EAST, even)
    put(EAST + 1, odd)
    for place, source in ((EDGE_LOW, north_left), (EDGE_HIGH, north)):
        pair = [rows(source, i, 2)[:, LANES - 1 :] for i in range(2)]
        put(place, jnp.where(low_half, pair[0], pair[1]))
    for i in range(2):
        put(NORTH + i, rows(north, i, 2))
        put(KAPPA + i, rows(kappa, i, 2))
        growth = jnp.exp(0.0633 * (rows(temp, i, 2) - 15.0)) * (
            1.0 + 0.25 * (rows(salt, i, 2) - 35.0)
        )
        put(GROWTH + i, growth)


def wet_masks(tally):
    level = row_index()
    return [level < tally[i : i + 1, :] for i in range(2)]


def mask_and_edges(amounts, tally, conc, first, last):
    lane = lane_index()
    wet = wet_masks(tally)
    low, high = (jnp.zeros((LEV, LANES), jnp.float32), jnp.zeros((LEV, LANES), jnp.float32))
    for t in range(NTR):
        for i in range(2):
            value = jnp.where(wet[i], rows(amounts, t * BLOCK + i, 2), 0.0)
            conc[t * BLOCK + i * LEV : t * BLOCK + (i + 1) * LEV, :] = value
            place = 64 * i + 2 * t
            here = (lane == place) | (lane == place + 1)
            low = jnp.where(here, pltpu.roll(value, place, 1) if place else value, low)
            high = jnp.where(here, pltpu.roll(value, place + 2, 1), high)
    first[...] = low
    last[...] = high


def face(courant):
    positive = courant >= 0
    weight = jnp.where(positive, 0.5 * (1.0 - courant), -0.5 * (1.0 + courant))
    return courant, positive, weight


def flux(edge, low, high, slope_low, slope_high):
    courant, positive, weight = edge
    return courant * (
        jnp.where(positive, low, high) + weight * jnp.where(positive, slope_low, slope_high)
    )


def advect_and_heat(
    chem, conc, below, above, left, right, own_first, own_last, fields, tally,
    moved, heat, ratios, inverses, links, couple, source, answer,
):
    lane = lane_index()
    level = row_index()
    wet = wet_masks(tally)
    wet_f = [w.astype(jnp.float32) for w in wet]
    wet_below = (below[LEV : 2 * LEV, :] > 0).astype(jnp.float32)
    wet_above = (above[0:LEV, :] > 0).astype(jnp.float32)

    def field(place):
        return rows(fields, place, ROWS)

    x_faces = [
        face(field(EAST_LOW) * wet_below * wet_f[0]),
        face(field(EAST) * wet_f[0] * wet_f[1]),
        face(field(EAST + 1) * wet_f[1] * wet_above),
    ]
    at_last, at_first = (lane == LANES - 1, lane == 0)
    y_faces = []
    for i in range(2):
        y_faces.append(face(field(NORTH + i) * wet_f[i] * pltpu.roll(wet_f[i], LANES - 1, 1)))

    def second(packed):
        return pltpu.roll(packed, LANES - 1, 1)

    def edge_flux(courant, lower, upper):
        far_low, near_low = (lower, second(lower))
        near_high, far_high = (upper, second(upper))
        step_low, step, step_high = (near_low - far_low, near_high - near_low, far_high - near_high)
        open_face = ((near_low > 0) & (near_high > 0)).astype(jnp.float32)
        return (
            flux(
                face(courant * open_face), near_low, near_high,
                minmod(step_low, step), minmod(step, step_high),
            ),
            step,
        )

    flux_first, step_first = edge_flux(field(EDGE_LOW), left[...], own_first[...])
    flux_last, unused = edge_flux(field(EDGE_HIGH), own_last[...], right[...])
    odd_lane = lane % 2 == 1
    patch_steps = jnp.where(odd_lane, pltpu.roll(right[...], 1, 1), step_first)
    patch_flux = jnp.where(odd_lane, pltpu.roll(flux_first, 1, 1), flux_last)

    mixture = [jnp.zeros((LEV, LANES), jnp.float32) for i in range(2)]
    for t in range(NTR):
        base = t * BLOCK
        far_low, near_low = (below[base : base + LEV, :], below[base + LEV : base + BLOCK, :])
        cells = [conc[base : base + LEV, :], conc[base + LEV : base + BLOCK, :]]
        near_high, far_high = (above[base : base + LEV, :], above[base + LEV : base + BLOCK, :])
        line = [far_low, near_low, cells[0], cells[1], near_high, far_high]
        steps = [line[n + 1] - line[n] for n in range(5)]
        slopes = [minmod(steps[n], steps[n + 1]) for n in range(4)]
        x_flux = [
            flux(x_faces[n], line[n + 1], line[n + 2], slopes[n], slopes[n + 1]) for n in range(3)
        ]
        weight = chem[0, t]
        for i in range(2):
            here = cells[i]
            turn = (LANES - (64 * i + 2 * t) - 1) % LANES
            steps_patch = pltpu.roll(patch_steps, turn, 1) if turn else patch_steps
            flux_patch = pltpu.roll(patch_flux, turn, 1) if turn else patch_flux
            following = pltpu.roll(jnp.where(at_first, steps_patch, here), LANES - 1, 1)
            step = following - here
            step_before = pltpu.roll(jnp.where(at_last, steps_patch, step), 1, 1)
            slope = minmod(step_before, step)
            upper = flux(y_faces[i], here, following, slope, pltpu.roll(slope, LANES - 1, 1))
            upper = jnp.where(at_last, flux_patch, upper)
            lower = jnp.where(at_first, flux_patch, pltpu.roll(upper, 1, 1))
            value = here + (x_flux[i] - x_flux[i + 1]) + (lower - upper)
            moved[base + i * LEV : base + (i + 1) * LEV, :] = value
            mixture[i] = mixture[i] + weight * value

    for i in range(2):
        next_wet = jnp.where(level == LEV - 1, 0.0, pltpu.roll(wet_f[i], LEV - 1, 0))
        coupling = field(KAPPA + i) * wet_f[i] * next_wet
        for r in range(i, 8, 2):
            couple[pl.ds(r, LEV, stride=8), :] = coupling
            source[pl.ds(r, LEV, stride=8), :] = (
                moved[i * LEV : (i + 1) * LEV, :] if r < 2 else mixture[i]
            )
    zero = jnp.zeros((8, LANES), jnp.float32)
    upper_link, ratio, carried = (zero, zero, zero)
    for k in range(LEV):
        at = slice(8 * k, 8 * k + 8)
        coupling = couple[at, :]
        inverse = 1.0 / (1.0 + upper_link + coupling + upper_link * ratio)
        ratio = -coupling * inverse
        carried = (source[at, :] + upper_link * carried) * inverse
        ratios[at, :] = ratio
        inverses[at, :] = inverse
        links[at, :] = upper_link * inverse
        answer[at, :] = carried
        upper_link = coupling
    solved = zero
    for k in reversed(range(LEV)):
        at = slice(8 * k, 8 * k + 8)
        solved = answer[at, :] - ratios[at, :] * solved
        answer[at, :] = solved
    for i in range(2):
        tracer, mixed = (rows(answer, i, 8), rows(answer, 2 + i, 8))
        advanced = tracer + 0.2 * field(GROWTH + i) * mixed
        absorption = jnp.where(wet[i], 0.02 + 0.04 * jnp.maximum(advanced, 0.0), 0.0)
        depth = absorption
        for shift in (1, 2, 4, 8):
            depth = depth + jnp.where(level >= shift, pltpu.roll(depth, shift, 0), 0.0)
        depth = depth - absorption
        heat[pl.ds(i, LEV, stride=2), :] = (
            16.0 * jnp.exp(-depth) * (1.0 - jnp.exp(-absorption))
        )


def mix_and_react(chem, moved, ratios, inverses, links, fields, tally, out, work, rate):
    shape = (NTR, LANES)
    wet = wet_masks(tally)
    for i in range(2):
        carried = jnp.zeros(shape, jnp.float32)
        for k in range(LEV):
            row = slice(8 * k + i, 8 * k + i + 1)
            at = pl.ds(i * LEV + k, NTR, stride=BLOCK)
            carried = moved[at, :] * inverses[row, :] + links[row, :] * carried
            work[at, :] = carried
        solved = jnp.zeros(shape, jnp.float32)
        for k in reversed(range(LEV)):
            row = slice(8 * k + i, 8 * k + i + 1)
            at = pl.ds(i * LEV + k, NTR, stride=BLOCK)
            solved = work[at, :] - ratios[row, :] * solved
            work[at, :] = solved
        rate[i * LEV : (i + 1) * LEV, :] = 0.2 * rows(fields, GROWTH + i, ROWS)
    for i in range(2):
        for half in range(2):
            start = i * LEV + 8 * half
            values = [work[t * BLOCK + start : t * BLOCK + start + 8, :] for t in range(NTR)]
            speed = rate[start : start + 8, :]
            is_wet = wet[i][8 * half : 8 * half + 8, :]
            for t in range(NTR):
                total = chem[t, 0] * values[0]
                for j in range(1, NTR):
                    total = total + chem[t, j] * values[j]
                out[pl.ds(t * BLOCK + 16 * half + i, 8, stride=2), :] = jnp.where(
                    is_wet, values[t] + speed * total, 0.0
                )


def shape_of(count):
    return pltpu.VMEM((count, LANES), jnp.float32)


def body(
    solute_amounts,
    submerged_layer_tally,
    zonal_boundary_transport,
    meridional_boundary_transport,
    diffusion_factor,
    thermal_state,
    saltiness_field,
    chemistry_matrix,
):
    sects = lax.axis_size("sect")
    across = ("tx", "ty")
    strips = lax.axis_size(across)
    smem = pl.BlockSpec(memory_space=pltpu.SMEM)
    vmem = pl.BlockSpec(memory_space=pltpu.VMEM)

    def upward(array, axis, count):
        return lax.ppermute(array, axis, [(n, n + 1) for n in range(count - 1)])

    def downward(array, axis, count):
        return lax.ppermute(array, axis, [(n + 1, n) for n in range(count - 1)])

    def flat(array):
        return array.reshape(-1, LANES)

    def near(*arrays):
        return [pltpu.with_memory_space_constraint(array, pltpu.VMEM) for array in arrays]

    north = flat(meridional_boundary_transport)
    north_left = upward(north, across, strips)
    sent = pl.pallas_call(pack_fields, out_shape=shape_of(LEV * ROWS), name="pack_fields")(
        flat(zonal_boundary_transport), north, flat(diffusion_factor), flat(thermal_state),
        flat(saltiness_field), *near(north_left),
    )
    fields = flat(
        lax.all_to_all(
            sent.reshape(LEV, ROWS // 4, 4, LANES), "sect", split_axis=0, concat_axis=0, tiled=True
        )
    )
    conc, first, last = pl.pallas_call(
        mask_and_edges,
        out_shape=(shape_of(NTR * BLOCK), shape_of(LEV), shape_of(LEV)),
        name="mask_and_edges",
    )(*near(flat(solute_amounts), submerged_layer_tally))
    below = upward(conc, "sect", sects)
    above = downward(conc, "sect", sects)
    left = upward(last, across, strips)
    right = downward(first, across, strips)
    column = shape_of(8 * LEV)
    moved, heat, ratios, inverses, links = pl.pallas_call(
        advect_and_heat,
        out_shape=(shape_of(NTR * BLOCK), shape_of(BLOCK), column, column, column),
        in_specs=[smem] + [vmem] * 9,
        scratch_shapes=[pltpu.VMEM((8 * LEV, LANES), jnp.float32)] * 3,
        name="advect_and_heat",
    )(
        chemistry_matrix,
        *near(
            conc, below, above, left, right, first, last, fields, submerged_layer_tally
        ),
    )
    heating = lax.all_to_all(heat, "sect", split_axis=0, concat_axis=0, tiled=True)
    advanced = pl.pallas_call(
        mix_and_react,
        out_shape=jax.ShapeDtypeStruct((NTR * BLOCK, LANES), jnp.float32),
        in_specs=[smem] + [vmem] * 6,
        scratch_shapes=[
            pltpu.VMEM((NTR * BLOCK, LANES), jnp.float32),
            pltpu.VMEM((BLOCK, LANES), jnp.float32),
        ],
        name="mix_and_react",
    )(
        chemistry_matrix,
        *near(moved, ratios, inverses, links, fields, submerged_layer_tally),
    )
    return (
        advanced.reshape(solute_amounts.shape),
        heating.reshape(zonal_boundary_transport.shape),
    )


def solution(mesh):
    in_specs = (
        P(None, None, "sect", ("tx", "ty")),
        P("sect", ("tx", "ty")),
        P("sect", None, ("tx", "ty")),
        P("sect", None, ("tx", "ty")),
        P("sect", None, ("tx", "ty")),
        P("sect", None, ("tx", "ty")),
        P("sect", None, ("tx", "ty")),
        P(),
    )
    out_specs = (P(None, None, "sect", ("tx", "ty")), P("sect", None, ("tx", "ty")))
    return jax.shard_map(body, mesh=mesh, in_specs=in_specs, out_specs=out_specs, check_vma=False)
```

time: 182 us -> 74.5 us (0.41)
  the two profiles are of different devices: /device:TPU:32 before, /device:TPU:31 now
where the time goes in v1:
time: 74.5 us; the launch traced here: 73.9 us
  starting transfers between devices  50.1 us (67%)
  waiting for transfers between devices  14.6 us (20%)
  Pallas kernels  7.17 us (10%)
  local copies, waits for them, and re-layouts  1.27 us (2%)
    all_to_all x1, starting transfers between devices, body(): lax.all_to_all(sent.reshape(LEV, ROWS // 4, 4, LANES), 'sect', split_axis...  18.6 us
    ppermute x3, starting transfers between devices, upward(): return lax.ppermute(array, axis, [(n, n + 1) for n in range(count - 1)])  16.5 us
    all_to_all x1, starting transfers between devices, body(): lax.all_to_all(heat, 'sect', split_axis=0, concat_axis=0, tiled=True)  11.7 us
    all_to_all x1, waiting for transfers between devices, body(): lax.all_to_all(heat, 'sect', split_axis=0, concat_axis=0, tiled=True)  8.44 us
    ppermute x2, waiting for transfers between devices, downward(): return lax.ppermute(array, axis, [(n + 1, n) for n in range(count - 1)])  5.14 us
    ppermute x2, starting transfers between devices, downward(): return lax.ppermute(array, axis, [(n + 1, n) for n in range(count - 1)])  3.21 us
    pallas_call x1, Pallas kernels, body(): pl.pallas_call(mix_and_react, out_shape=jax.ShapeDtypeStruct((NTR * BLOCK...  2.96 us
    pallas_call x1, Pallas kernels, body(): pl.pallas_call(advect_and_heat, out_shape=(shape_of(NTR * BLOCK), shape_o...  2.49 us
  transfers between devices with their start and end apart: 7, of which 3 were waited for; matrix products, arithmetic and copies ran while one was open for 0% of the time, Pallas kernels for 4%

profile of v1, /device:TPU:31, one launch (start us, length us, event | category | flops | bytes accessed | tf_op | source)
XLA Modules:
  0.0 73.9 jit_solution(11810670098987398229)
XLA Ops:
  0.6 0.0 copy-start
  0.6 5.4 %collective-permute-start.4 = (f32[32,128]{1,0:T(8,128)}, f32[32,128]{1,0:T(8,128)S(1)}, u32[]{:S(2)}, u32[]{:S(2)}) collective-permute-start(f32[32,128]{1,0:T(8,128)} %bitcast.17), channel_id=1, source_target_pairs={{0,1},{1,2},{2,3},{3,4},{4,5},{5,6},{6,7},{7,8},{8,9},{9,10},{10,1... | collective-permute-start | bytes 49160 | tf_op jit(solution)/shard_map/ppermute | solution.py:257
  6.0 1.1 %collective-permute-done.4.north_left = f32[32,128]{1,0:T(8,128)S(1)} collective-permute-done((f32[32,128]{1,0:T(8,128)}, f32[32,128]{1,0:T(8,128)S(1)}, u32[]{:S(2)}, u32[]{:S(2)}) %collective-permute-start.4) | collective-permute-done | bytes 16416 | tf_op jit(solution)/shard_map/ppermute | solution.py:257
  7.1 1.5 %pack_fields.1 = f32[192,128]{1,0:T(8,128)} custom-call(f32[32,128]{1,0:T(8,128)} %bitcast.16, f32[32,128]{1,0:T(8,128)} %bitcast.18, f32[32,128]{1,0:T(8,128)} %bitcast.19, f32[32,128]{1,0:T(8,128)} %bitcast.20, f32[32,128]{1,0:T(8,128)} %bitcast.21, f32[32,128]{1,0:T(8,128)S(1)} %collective-permute-done.4.north_left), custom_call_target="tpu_custom_call" | custom-call | tf_op jit(solution)/shard_map/pack_fields/pallas_call | solution.py:270
  8.6 18.6 %all-to-all-start = ((f32[16,3,4,128]{3,2,1,0:T(4,128)}), f32[16,3,4,128]{3,2,1,0:T(4,128)S(1)}, u32[]{:S(2)}, u32[]{:S(2)}) async-start(f32[16,3,4,128]{3,2,1,0:T(4,128)} %bitcast.6), calls=%async_computation | async-start | bytes 196608 | tf_op jit(solution)/shard_map/all_to_all | solution.py:275
  27.2 0.0 copy-start.1
  27.2 0.0 copy-done
  27.2 0.7 copy-done.1
  27.9 0.2 mask_and_edges.1
  28.1 1.3 %collective-permute-start.1 = (f32[608,128]{1,0:T(8,128)S(1)}, f32[608,128]{1,0:T(8,128)S(1)}, u32[]{:S(2)}, u32[]{:S(2)}) collective-permute-start(f32[608,128]{1,0:T(8,128)S(1)} %get-tuple-element.10.conc), channel_id=1, source_target_pairs={{64,0},{128,64},{192,128},{256,192},{320,256},{384,320},{448,384},... | collective-permute-start | bytes 933896 | tf_op jit(solution)/shard_map/ppermute | solution.py:260
  29.4 4.0 %collective-permute-start = (f32[608,128]{1,0:T(8,128)S(1)}, f32[608,128]{1,0:T(8,128)S(1)}, u32[]{:S(2)}, u32[]{:S(2)}) collective-permute-start(f32[608,128]{1,0:T(8,128)S(1)} %get-tuple-element.10.conc), channel_id=1, source_target_pairs={{0,64},{64,128},{128,192},{192,256},{256,320},{320,384},{384,448},... | collective-permute-start | bytes 933896 | tf_op jit(solution)/shard_map/ppermute | solution.py:257
  33.4 7.2 %collective-permute-start.2 = (f32[16,128]{1,0:T(8,128)S(1)}, f32[16,128]{1,0:T(8,128)S(1)}, u32[]{:S(2)}, u32[]{:S(2)}) collective-permute-start(f32[16,128]{1,0:T(8,128)S(1)} %get-tuple-element.11.own_last), channel_id=1, source_target_pairs={{0,1},{1,2},{2,3},{3,4},{4,5},{5,6},{6,7},{7,8},{8,9},{9,10},{10,1... | collective-permute-start | bytes 24584 | tf_op jit(solution)/shard_map/ppermute | solution.py:257
  40.6 1.9 %collective-permute-start.3 = (f32[16,128]{1,0:T(8,128)S(1)}, f32[16,128]{1,0:T(8,128)S(1)}, u32[]{:S(2)}, u32[]{:S(2)}) collective-permute-start(f32[16,128]{1,0:T(8,128)S(1)} %get-tuple-element.12.own_first), channel_id=1, source_target_pairs={{1,0},{2,1},{3,2},{4,3},{5,4},{6,5},{7,6},{8,7},{9,8},{10,9},{11,1... | collective-permute-start | bytes 24584 | tf_op jit(solution)/shard_map/ppermute | solution.py:260
  42.5 0.0 collective-permute-done.2.left
  42.5 5.1 %collective-permute-done.3.right = f32[16,128]{1,0:T(8,128)S(1)} collective-permute-done((f32[16,128]{1,0:T(8,128)S(1)}, f32[16,128]{1,0:T(8,128)S(1)}, u32[]{:S(2)}, u32[]{:S(2)}) %collective-permute-start.3) | collective-permute-done | bytes 8224 | tf_op jit(solution)/shard_map/ppermute | solution.py:260
  47.6 0.0 collective-permute-done.1.above
  47.6 0.0 collective-permute-done.below
  47.6 0.0 all-to-all-done
  47.7 2.5 %advect_and_heat.1 = (f32[608,128]{1,0:T(8,128)S(1)}, f32[32,128]{1,0:T(8,128)}, f32[128,128]{1,0:T(8,128)S(1)}, f32[128,128]{1,0:T(8,128)S(1)}, f32[128,128]{1,0:T(8,128)S(1)}) custom-call(f32[19,19]{1,0:T(8,128)} %chem.3, f32[608,128]{1,0:T(8,128)S(1)} %get-tuple-element.10.conc, f32[608,128]{1,0:T(8,128)S(1)} %collective-permute-done.below, ...), custom_call_target="tpu_custom_call" | custom-call | tf_op jit(solution)/shard_map/advect_and_heat/pallas_call | solution.py:289
  50.1 11.7 %all-to-all-start.1 = ((f32[16,2,128]{2,1,0:T(2,128)}), f32[16,2,128]{2,1,0:T(2,128)S(1)}, u32[]{:S(2)}, u32[]{:S(2)}) async-start(f32[16,2,128]{2,1,0:T(2,128)} %bitcast.9), calls=%async_computation.1 | async-start | bytes 32768 | tf_op jit(solution)/shard_map/all_to_all | solution.py:301
  61.9 3.0 %mix_and_react.1 = f32[608,128]{1,0:T(8,128)} custom-call(f32[19,19]{1,0:T(8,128)} %chem.3, f32[608,128]{1,0:T(8,128)S(1)} %get-tuple-element.13.moved, f32[128,128]{1,0:T(8,128)S(1)} %get-tuple-element.14.ratios, f32[128,128]{1,0:T(8,128)S(1)} %get-tuple-element.15.inverses, f32[128,128]{1,0:T(8,128)S(1)} %get-tuple-element.16.links, ...), custom_call_target="tpu_custom_call" | custom-call | tf_op jit(solution)/shard_map/mix_and_react/pallas_call | solution.py:302
  64.8 8.4 %all-to-all-done.1 = f32[16,2,128]{2,1,0:T(2,128)S(1)} async-done(((f32[16,2,128]{2,1,0:T(2,128)}), f32[16,2,128]{2,1,0:T(2,128)S(1)}, u32[]{:S(2)}, u32[]{:S(2)}) %all-to-all-start.1) | async-done | bytes 16416 | tf_op jit(solution)/shard_map/all_to_all | solution.py:301
  73.3 0.6 copy.11
Async XLA Ops:
  0.6 26.6 %copy-start = (f32[19,16,2,128]{3,2,1,0:T(2,128)S(1)}, f32[19,16,2,128]{3,2,1,0:T(2,128)}, u32[]{:S(2)}) copy-start(f32[19,16,2,128]{3,2,1,0:T(2,128)} %param.8) | copy-start | bytes 933892
  0.6 6.4 %collective-permute-start.4 = (f32[32,128]{1,0:T(8,128)}, f32[32,128]{1,0:T(8,128)S(1)}, u32[]{:S(2)}, u32[]{:S(2)}) collective-permute-start(f32[32,128]{1,0:T(8,128)} %bitcast.17), channel_id=1, source_target_pairs={{0,1},{1,2},{2,3},{3,4},{4,5},{5,6},{6,7},{7,8},{8,9},{9,10},{10,1... | collective-permute-start | bytes 49160 | tf_op jit(solution)/shard_map/ppermute | solution.py:257
  8.6 39.1 %all-to-all-start = ((f32[16,3,4,128]{3,2,1,0:T(4,128)}), f32[16,3,4,128]{3,2,1,0:T(4,128)S(1)}, u32[]{:S(2)}, u32[]{:S(2)}) async-start(f32[16,3,4,128]{3,2,1,0:T(4,128)} %bitcast.6), calls=%async_computation | async-start | bytes 196608 | tf_op jit(solution)/shard_map/all_to_all | solution.py:275
  27.2 0.7 copy-start.1
  28.1 19.6 %collective-permute-start.1 = (f32[608,128]{1,0:T(8,128)S(1)}, f32[608,128]{1,0:T(8,128)S(1)}, u32[]{:S(2)}, u32[]{:S(2)}) collective-permute-start(f32[608,128]{1,0:T(8,128)S(1)} %get-tuple-element.10.conc), channel_id=1, source_target_pairs={{64,0},{128,64},{192,128},{256,192},{320,256},{384,320},{448,384},... | collective-permute-start | bytes 933896 | tf_op jit(solution)/shard_map/ppermute | solution.py:260
  29.4 18.3 %collective-permute-start = (f32[608,128]{1,0:T(8,128)S(1)}, f32[608,128]{1,0:T(8,128)S(1)}, u32[]{:S(2)}, u32[]{:S(2)}) collective-permute-start(f32[608,128]{1,0:T(8,128)S(1)} %get-tuple-element.10.conc), channel_id=1, source_target_pairs={{0,64},{64,128},{128,192},{192,256},{256,320},{320,384},{384,448},... | collective-permute-start | bytes 933896 | tf_op jit(solution)/shard_map/ppermute | solution.py:257
  33.4 9.1 %collective-permute-start.2 = (f32[16,128]{1,0:T(8,128)S(1)}, f32[16,128]{1,0:T(8,128)S(1)}, u32[]{:S(2)}, u32[]{:S(2)}) collective-permute-start(f32[16,128]{1,0:T(8,128)S(1)} %get-tuple-element.11.own_last), channel_id=1, source_target_pairs={{0,1},{1,2},{2,3},{3,4},{4,5},{5,6},{6,7},{7,8},{8,9},{9,10},{10,1... | collective-permute-start | bytes 24584 | tf_op jit(solution)/shard_map/ppermute | solution.py:257
  40.6 7.1 %collective-permute-start.3 = (f32[16,128]{1,0:T(8,128)S(1)}, f32[16,128]{1,0:T(8,128)S(1)}, u32[]{:S(2)}, u32[]{:S(2)}) collective-permute-start(f32[16,128]{1,0:T(8,128)S(1)} %get-tuple-element.12.own_first), channel_id=1, source_target_pairs={{1,0},{2,1},{3,2},{4,3},{5,4},{6,5},{7,6},{8,7},{9,8},{10,9},{11,1... | collective-permute-start | bytes 24584 | tf_op jit(solution)/shard_map/ppermute | solution.py:260
  50.1 23.1 %all-to-all-start.1 = ((f32[16,2,128]{2,1,0:T(2,128)}), f32[16,2,128]{2,1,0:T(2,128)S(1)}, u32[]{:S(2)}, u32[]{:S(2)}) async-start(f32[16,2,128]{2,1,0:T(2,128)} %bitcast.9), calls=%async_computation.1 | async-start | bytes 32768 | tf_op jit(solution)/shard_map/all_to_all | solution.py:301

commit v2 on v1

--- a/solution.py
+++ b/solution.py
@@ -5,12 +5,15 @@
 from jax.experimental.pallas import tpu as pltpu
 from jax.sharding import PartitionSpec as P
 
+
 NTR = 19
 LEV = 16
 LANES = 128
 BLOCK = 2 * LEV
 ROWS = 12
 EAST_LOW, EAST, NORTH, EDGE_LOW, EDGE_HIGH, KAPPA, GROWTH = 0, 1, 3, 5, 6, 7, 9
+FIELD_ROOT = 12
+HEAT_ROOT = 8
 
 
 def lane_index():
@@ -23,6 +26,10 @@
 
 def rows(ref, start, stride):
     return ref[pl.ds(start, LEV, stride=stride), :]
+
+
+def rotate(value, root):
+    return pltpu.roll(value, (LEV - root) % LEV, 0) if root % LEV else value
 
 
 def minmod(first, second):
@@ -31,19 +38,23 @@
     )
 
 
-def pack_fields(east, north, kappa, temp, salt, north_left, out):
+def prepare(
+    amounts, tally, east, north, kappa, temp, salt, conc, sent, near_swap, far_swap, first, last, wet
+):
     def put(place, value):
-        out[pl.ds(place, LEV, stride=ROWS), :] = value
-
-    put(ROWS - 1, jnp.zeros((LEV, LANES), jnp.float32))
-    low_half = lane_index() < LANES // 2
+        sent[pl.ds(place, LEV, stride=ROWS), :] = rotate(value, FIELD_ROOT)
+
+    lane = lane_index()
+    level = row_index()
     even, odd = (rows(east, 0, 2), rows(east, 1, 2))
-    put(EAST_LOW, jnp.where(row_index() == 0, 0.0, pltpu.roll(odd, 1, 0)))
+    put(EAST_LOW, jnp.where(level == 0, 0.0, pltpu.roll(odd, 1, 0)))
     put(EAST, even)
     put(EAST + 1, odd)
-    for place, source in ((EDGE_LOW, north_left), (EDGE_HIGH, north)):
-        pair = [rows(source, i, 2)[:, LANES - 1 :] for i in range(2)]
-        put(place, jnp.where(low_half, pair[0], pair[1]))
+    pair = [rows(north, i, 2)[:, LANES - 1 :] for i in range(2)]
+    edge = jnp.where(lane < LANES // 2, pair[0], pair[1])
+    put(EDGE_HIGH, edge)
+    for place in (EDGE_LOW, ROWS - 1):
+        put(place, jnp.zeros((LEV, LANES), jnp.float32))
     for i in range(2):
         put(NORTH + i, rows(north, i, 2))
         put(KAPPA + i, rows(kappa, i, 2))
@@ -51,20 +62,11 @@
             1.0 + 0.25 * (rows(salt, i, 2) - 35.0)
         )
         put(GROWTH + i, growth)
-
-
-def wet_masks(tally):
-    level = row_index()
-    return [level < tally[i : i + 1, :] for i in range(2)]
-
-
-def mask_and_edges(amounts, tally, conc, first, last):
-    lane = lane_index()
-    wet = wet_masks(tally)
+    is_wet = [level < tally[i : i + 1, :] for i in range(2)]
     low, high = (jnp.zeros((LEV, LANES), jnp.float32), jnp.zeros((LEV, LANES), jnp.float32))
     for t in range(NTR):
         for i in range(2):
-            value = jnp.where(wet[i], rows(amounts, t * BLOCK + i, 2), 0.0)
+            value = jnp.where(is_wet[i], rows(amounts, t * BLOCK + i, 2), 0.0)
             conc[t * BLOCK + i * LEV : t * BLOCK + (i + 1) * LEV, :] = value
             place = 64 * i + 2 * t
             here = (lane == place) | (lane == place + 1)
@@ -72,6 +74,31 @@
             high = jnp.where(here, pltpu.roll(value, place + 2, 1), high)
     first[...] = low
     last[...] = high
+    for i in range(2):
+        wet[i * LEV : (i + 1) * LEV, :] = is_wet[i].astype(jnp.float32)
+    is_even = even_strip()
+    near_swap[:LEV, :] = jnp.where(is_even, high, low)
+    near_swap[LEV:, :] = edge
+    far_swap[:LEV, :] = jnp.where(is_even, low, high)
+    far_swap[LEV:, :] = edge
+
+
+def even_strip():
+    return lax.axis_index("ty") % 2 == 0
+
+
+def from_left(near_got, far_got, part):
+    return jnp.where(even_strip(), far_got[part, :], near_got[part, :])
+
+
+def from_right(near_got, far_got, part):
+    return jnp.where(even_strip(), near_got[part, :], far_got[part, :])
+
+
+def add_left_edge(sent, near_got, far_got, out):
+    out[...] = sent[...]
+    edge = from_left(near_got, far_got, slice(LEV, 2 * LEV))
+    out[pl.ds(EDGE_LOW, LEV, stride=ROWS), :] = rotate(edge, FIELD_ROOT)
 
 
 def face(courant):
@@ -88,18 +115,19 @@
 
 
 def advect_and_heat(
-    chem, conc, below, above, left, right, own_first, own_last, fields, tally,
-    moved, heat, ratios, inverses, links, couple, source, answer,
+    chem, conc, below, above, near_got, far_got, own_first, own_last, fields, wet,
+    moved, heat, ratios, inverses, links, rate, couple, source, answer,
 ):
     lane = lane_index()
     level = row_index()
-    wet = wet_masks(tally)
-    wet_f = [w.astype(jnp.float32) for w in wet]
+    wet_f = [wet[i * LEV : (i + 1) * LEV, :] for i in range(2)]
+    left = from_left(near_got, far_got, slice(0, LEV))
+    right = from_right(near_got, far_got, slice(0, LEV))
     wet_below = (below[LEV : 2 * LEV, :] > 0).astype(jnp.float32)
     wet_above = (above[0:LEV, :] > 0).astype(jnp.float32)
 
     def field(place):
-        return rows(fields, place, ROWS)
+        return rotate(rows(fields, place, ROWS), LEV - FIELD_ROOT)
 
     x_faces = [
         face(field(EAST_LOW) * wet_below * wet_f[0]),
@@ -127,13 +155,13 @@
             step,
         )
 
-    flux_first, step_first = edge_flux(field(EDGE_LOW), left[...], own_first[...])
-    flux_last, unused = edge_flux(field(EDGE_HIGH), own_last[...], right[...])
+    flux_first, step_first = edge_flux(field(EDGE_LOW), left, own_first[...])
+    flux_last, _ = edge_flux(field(EDGE_HIGH), own_last[...], right)
     odd_lane = lane % 2 == 1
-    patch_steps = jnp.where(odd_lane, pltpu.roll(right[...], 1, 1), step_first)
+    patch_steps = jnp.where(odd_lane, pltpu.roll(right, 1, 1), step_first)
     patch_flux = jnp.where(odd_lane, pltpu.roll(flux_first, 1, 1), flux_last)
 
-    mixture = [jnp.zeros((LEV, LANES), jnp.float32) for i in range(2)]
+    mixture = [jnp.zeros((LEV, LANES), jnp.float32) for _ in range(2)]
     for t in range(NTR):
         base = t * BLOCK
         far_low, near_low = (below[base : base + LEV, :], below[base + LEV : base + BLOCK, :])
@@ -189,21 +217,21 @@
         solved = answer[at, :] - ratios[at, :] * solved
         answer[at, :] = solved
     for i in range(2):
+        rate[i * LEV : (i + 1) * LEV, :] = 0.2 * field(GROWTH + i)
         tracer, mixed = (rows(answer, i, 8), rows(answer, 2 + i, 8))
-        advanced = tracer + 0.2 * field(GROWTH + i) * mixed
-        absorption = jnp.where(wet[i], 0.02 + 0.04 * jnp.maximum(advanced, 0.0), 0.0)
+        advanced = wet_f[i] * (tracer + rate[i * LEV : (i + 1) * LEV, :] * mixed)
+        absorption = wet_f[i] * (0.02 + 0.04 * jnp.maximum(advanced, 0.0))
         depth = absorption
         for shift in (1, 2, 4, 8):
             depth = depth + jnp.where(level >= shift, pltpu.roll(depth, shift, 0), 0.0)
         depth = depth - absorption
-        heat[pl.ds(i, LEV, stride=2), :] = (
-            16.0 * jnp.exp(-depth) * (1.0 - jnp.exp(-absorption))
+        heat[pl.ds(i, LEV, stride=2), :] = rotate(
+            16.0 * jnp.exp(-depth) * (1.0 - jnp.exp(-absorption)), HEAT_ROOT
         )
 
 
-def mix_and_react(chem, moved, ratios, inverses, links, fields, tally, out, work, rate):
+def mix_and_react(chem, moved, ratios, inverses, links, rate, wet, out, work):
     shape = (NTR, LANES)
-    wet = wet_masks(tally)
     for i in range(2):
         carried = jnp.zeros(shape, jnp.float32)
         for k in range(LEV):
@@ -217,19 +245,18 @@
             at = pl.ds(i * LEV + k, NTR, stride=BLOCK)
             solved = work[at, :] - ratios[row, :] * solved
             work[at, :] = solved
-        rate[i * LEV : (i + 1) * LEV, :] = 0.2 * rows(fields, GROWTH + i, ROWS)
     for i in range(2):
         for half in range(2):
             start = i * LEV + 8 * half
             values = [work[t * BLOCK + start : t * BLOCK + start + 8, :] for t in range(NTR)]
             speed = rate[start : start + 8, :]
-            is_wet = wet[i][8 * half : 8 * half + 8, :]
+            is_wet = wet[start : start + 8, :]
             for t in range(NTR):
                 total = chem[t, 0] * values[0]
                 for j in range(1, NTR):
                     total = total + chem[t, j] * values[j]
-                out[pl.ds(t * BLOCK + 16 * half + i, 8, stride=2), :] = jnp.where(
-                    is_wet, values[t] + speed * total, 0.0
+                out[pl.ds(t * BLOCK + 16 * half + i, 8, stride=2), :] = is_wet * (
+                    values[t] + speed * total
                 )
 
 
@@ -265,53 +292,63 @@
     def near(*arrays):
         return [pltpu.with_memory_space_constraint(array, pltpu.VMEM) for array in arrays]
 
-    north = flat(meridional_boundary_transport)
-    north_left = upward(north, across, strips)
-    sent = pl.pallas_call(pack_fields, out_shape=shape_of(LEV * ROWS), name="pack_fields")(
-        flat(zonal_boundary_transport), north, flat(diffusion_factor), flat(thermal_state),
-        flat(saltiness_field), *near(north_left),
-    )
-    fields = flat(
-        lax.all_to_all(
-            sent.reshape(LEV, ROWS // 4, 4, LANES), "sect", split_axis=0, concat_axis=0, tiled=True
+    def exchange(array, root):
+        group = [(root + n) % sects for n in range(sects)]
+        return lax.all_to_all(
+            array, "sect", split_axis=0, concat_axis=0, tiled=True,
+            axis_index_groups=[group] if root else None,
         )
-    )
-    conc, first, last = pl.pallas_call(
-        mask_and_edges,
-        out_shape=(shape_of(NTR * BLOCK), shape_of(LEV), shape_of(LEV)),
-        name="mask_and_edges",
-    )(*near(flat(solute_amounts), submerged_layer_tally))
+
+    def swap(array, start):
+        pairs = [(n, n + 1) for n in range(start, strips - 1, 2)]
+        return lax.ppermute(array, across, pairs + [(high, low) for low, high in pairs])
+
+    tile, half = (shape_of(NTR * BLOCK), shape_of(LEV))
+    conc, sent, near_swap, far_swap, first, last, wet = pl.pallas_call(
+        prepare,
+        out_shape=(
+            tile, shape_of(LEV * ROWS), shape_of(BLOCK), shape_of(BLOCK), half, half,
+            shape_of(BLOCK),
+        ),
+        name="prepare",
+    )(
+        flat(solute_amounts), submerged_layer_tally, flat(zonal_boundary_transport),
+        flat(meridional_boundary_transport), flat(diffusion_factor), flat(thermal_state),
+        flat(saltiness_field),
+    )
+    far_got = swap(far_swap, 1)
+    near_got = swap(near_swap, 0)
     below = upward(conc, "sect", sects)
     above = downward(conc, "sect", sects)
-    left = upward(last, across, strips)
-    right = downward(first, across, strips)
+    sent = pl.pallas_call(
+        add_left_edge,
+        out_shape=jax.ShapeDtypeStruct((LEV * ROWS, LANES), jnp.float32),
+        name="add_left_edge",
+    )(*near(sent, near_got, far_got))
+    fields = exchange(sent.reshape(LEV, ROWS // 4, 4, LANES), FIELD_ROOT)
+    fields = flat(fields)
     column = shape_of(8 * LEV)
-    moved, heat, ratios, inverses, links = pl.pallas_call(
+    moved, heat, ratios, inverses, links, rate = pl.pallas_call(
         advect_and_heat,
-        out_shape=(shape_of(NTR * BLOCK), shape_of(BLOCK), column, column, column),
+        out_shape=(tile, shape_of(BLOCK), column, column, column, shape_of(BLOCK)),
         in_specs=[smem] + [vmem] * 9,
         scratch_shapes=[pltpu.VMEM((8 * LEV, LANES), jnp.float32)] * 3,
         name="advect_and_heat",
     )(
         chemistry_matrix,
-        *near(
-            conc, below, above, left, right, first, last, fields, submerged_layer_tally
-        ),
-    )
-    heating = lax.all_to_all(heat, "sect", split_axis=0, concat_axis=0, tiled=True)
+        *near(conc, below, above, near_got, far_got, first, last, fields, wet),
+    )
+    heating = flat(exchange(heat.reshape(LEV, 2, LANES), HEAT_ROOT))
+    turn = 2 * HEAT_ROOT % BLOCK
+    if turn:
+        heating = jnp.concatenate([heating[BLOCK - turn :], heating[: BLOCK - turn]])
     advanced = pl.pallas_call(
         mix_and_react,
         out_shape=jax.ShapeDtypeStruct((NTR * BLOCK, LANES), jnp.float32),
         in_specs=[smem] + [vmem] * 6,
-        scratch_shapes=[
-            pltpu.VMEM((NTR * BLOCK, LANES), jnp.float32),
-            pltpu.VMEM((BLOCK, LANES), jnp.float32),
-        ],
+        scratch_shapes=[pltpu.VMEM((NTR * BLOCK, LANES), jnp.float32)],
         name="mix_and_react",
-    )(
-        chemistry_matrix,
-        *near(moved, ratios, inverses, links, fields, submerged_layer_tally),
-    )
+    )(chemistry_matrix, *near(moved, ratios, inverses, links, rate, wet))
     return (
         advanced.reshape(solute_amounts.shape),
         heating.reshape(zonal_boundary_transport.shape),
@@ -330,4 +367,5 @@
         P(),
     )
     out_specs = (P(None, None, "sect", ("tx", "ty")), P("sect", None, ("tx", "ty")))
+
     return jax.shard_map(body, mesh=mesh, in_specs=in_specs, out_specs=out_specs, check_vma=False)

time: 74.5 us -> 64.4 us (0.86)
  the two profiles are of different devices: /device:TPU:31 before, /device:TPU:6 now
where the time goes in v2:
time: 64.4 us; the launch traced here: 63.8 us
  starting transfers between devices  44.8 us (70%)
  waiting for transfers between devices  10.4 us (16%)
  Pallas kernels  7.29 us (11%)
  between operations  0.68 us (1%)
    all_to_all x2, starting transfers between devices, exchange(): lax.all_to_all(array, 'sect', split_axis=0, concat_axis=0, tiled=True, ax...  34.2 us
    ppermute x1, waiting for transfers between devices, downward(): return lax.ppermute(array, axis, [(n + 1, n) for n in range(count - 1)])  8.23 us
    ppermute x2, starting transfers between devices, swap(): lax.ppermute(array, across, pairs + [(high, low) for low, high in pairs])  4.76 us
    ppermute x1, starting transfers between devices, upward(): return lax.ppermute(array, axis, [(n, n + 1) for n in range(count - 1)])  4.57 us
    pallas_call x1, Pallas kernels, body(): pl.pallas_call(mix_and_react, out_shape=jax.ShapeDtypeStruct((NTR * BLOCK...  2.95 us
    pallas_call x1, Pallas kernels, body(): pl.pallas_call(advect_and_heat, out_shape=(tile, shape_of(BLOCK), column,...  2.44 us
    ppermute x2, waiting for transfers between devices, swap(): lax.ppermute(array, across, pairs + [(high, low) for low, high in pairs])  2.2 us
  transfers between devices with their start and end apart: 6, of which 2 were waited for; matrix products, arithmetic and copies ran while one was open for 0% of the time, Pallas kernels for 5%

profile of v2, /device:TPU:6, one launch (start us, length us, event | category | flops | bytes accessed | tf_op | source)
XLA Modules:
  0.0 63.8 jit_solution(16950620021361966103)
XLA Ops:
  0.6 1.3 %prepare.1 = (f32[608,128]{1,0:T(8,128)S(1)}, f32[192,128]{1,0:T(8,128)S(1)}, f32[32,128]{1,0:T(8,128)S(1)}, f32[32,128]{1,0:T(8,128)S(1)}, f32[16,128]{1,0:T(8,...) custom-call(f32[608,128]{1,0:T(8,128)} %bitcast.16, s32[2,128]{1,0:T(2,128)} %tally.1, f32[32,128]{1,0:T(8,128)} %bitcast.20, ...), custom_call_target="tpu_custom_call" | custom-call | tf_op jit(solution)/shard_map/prepare/pallas_call | solution.py:307
  1.9 1.9 %collective-permute-start.2 = (f32[32,128]{1,0:T(8,128)S(1)}, f32[32,128]{1,0:T(8,128)S(1)}, u32[]{:S(2)}, u32[]{:S(2)}) collective-permute-start(f32[32,128]{1,0:T(8,128)S(1)} %get-tuple-element.16), channel_id=1, source_target_pairs={{0,1},{2,3},{4,5},{6,7},{8,9},{10,11},{12,13},{14,15},{16,17},{18,... | collective-permute-start | bytes 49160 | tf_op jit(solution)/shard_map/ppermute | solution.py:304
  3.8 2.8 %collective-permute-start.3 = (f32[32,128]{1,0:T(8,128)S(1)}, f32[32,128]{1,0:T(8,128)S(1)}, u32[]{:S(2)}, u32[]{:S(2)}) collective-permute-start(f32[32,128]{1,0:T(8,128)S(1)} %get-tuple-element.17), channel_id=1, source_target_pairs={{1,2},{3,4},{5,6},{7,8},{9,10},{11,12},{13,14},{15,16},{17,18},{19... | collective-permute-start | bytes 49160 | tf_op jit(solution)/shard_map/ppermute | solution.py:304
  6.7 0.0 collective-permute-done.2.near_got
  6.7 2.2 %collective-permute-done.3.far_got = f32[32,128]{1,0:T(8,128)S(1)} collective-permute-done((f32[32,128]{1,0:T(8,128)S(1)}, f32[32,128]{1,0:T(8,128)S(1)}, u32[]{:S(2)}, u32[]{:S(2)}) %collective-permute-start.3) | collective-permute-done | bytes 16416 | tf_op jit(solution)/shard_map/ppermute | solution.py:304
  8.9 0.7 %add_left_edge.1 = f32[192,128]{1,0:T(8,128)} custom-call(f32[192,128]{1,0:T(8,128)S(1)} %get-tuple-element.20.sent, f32[32,128]{1,0:T(8,128)S(1)} %collective-permute-done.2.near_got, f32[32,128]{1,0:T(8,128)S(1)} %collective-permute-done.3.far_got), custom_call_target="tpu_custom_call" | custom-call | tf_op jit(solution)/shard_map/add_left_edge/pallas_call | solution.py:323
  9.5 20.9 %all-to-all-start = ((f32[16,3,4,128]{3,2,1,0:T(4,128)}), f32[16,3,4,128]{3,2,1,0:T(4,128)S(1)}, u32[]{:S(2)}, u32[]{:S(2)}) async-start(f32[16,3,4,128]{3,2,1,0:T(4,128)} %bitcast.15), calls=%async_computation | async-start | bytes 196608 | tf_op jit(solution)/shard_map/all_to_all | solution.py:297
  30.4 1.3 %collective-permute-start.1 = (f32[608,128]{1,0:T(8,128)S(1)}, f32[608,128]{1,0:T(8,128)S(1)}, u32[]{:S(2)}, u32[]{:S(2)}) collective-permute-start(f32[608,128]{1,0:T(8,128)S(1)} %get-tuple-element.15.conc), channel_id=1, source_target_pairs={{64,0},{128,64},{192,128},{256,192},{320,256},{384,320},{448,384},... | collective-permute-start | bytes 933896 | tf_op jit(solution)/shard_map/ppermute | solution.py:287
  31.7 4.6 %collective-permute-start = (f32[608,128]{1,0:T(8,128)S(1)}, f32[608,128]{1,0:T(8,128)S(1)}, u32[]{:S(2)}, u32[]{:S(2)}) collective-permute-start(f32[608,128]{1,0:T(8,128)S(1)} %get-tuple-element.15.conc), channel_id=1, source_target_pairs={{0,64},{64,128},{128,192},{192,256},{256,320},{320,384},{384,448},... | collective-permute-start | bytes 933896 | tf_op jit(solution)/shard_map/ppermute | solution.py:284
  36.3 8.2 %collective-permute-done.1.above = f32[608,128]{1,0:T(8,128)S(1)} collective-permute-done((f32[608,128]{1,0:T(8,128)S(1)}, f32[608,128]{1,0:T(8,128)S(1)}, u32[]{:S(2)}, u32[]{:S(2)}) %collective-permute-start.1) | collective-permute-done | bytes 311328 | tf_op jit(solution)/shard_map/ppermute | solution.py:287
  44.5 0.0 collective-permute-done.below
  44.5 0.0 all-to-all-done
  44.5 2.4 %advect_and_heat.1 = (f32[608,128]{1,0:T(8,128)S(1)}, f32[32,128]{1,0:T(8,128)}, f32[128,128]{1,0:T(8,128)S(1)}, f32[128,128]{1,0:T(8,128)S(1)}, f32[128,128]{1,0:T(8,128)S(1)}, /*index=5*/f32[32,128]{1,0:T(8,128)S(1)}) custom-call(f32[19,19]{1,0:T(8,128)} %chem.3, f32[608,128]{1,0:T(8,128)S(1)} %get-tuple-element.15.conc, ...), custom_call_target="tpu_custom_call" | custom-call | tf_op jit(solution)/shard_map/advect_and_heat/pallas_call | solution.py:331
  46.9 13.3 %all-to-all-start.1 = ((f32[16,2,128]{2,1,0:T(2,128)}), f32[16,2,128]{2,1,0:T(2,128)S(1)}, u32[]{:S(2)}, u32[]{:S(2)}) async-start(f32[16,2,128]{2,1,0:T(2,128)} %bitcast.9), calls=%async_computation.1 | async-start | bytes 32768 | tf_op jit(solution)/shard_map/all_to_all | solution.py:297
  60.3 2.9 %mix_and_react.1 = f32[608,128]{1,0:T(8,128)} custom-call(f32[19,19]{1,0:T(8,128)} %chem.3, f32[608,128]{1,0:T(8,128)S(1)} %get-tuple-element.22.moved, f32[128,128]{1,0:T(8,128)S(1)} %get-tuple-element.23.ratios, f32[128,128]{1,0:T(8,128)S(1)} %get-tuple-element.24.inverses, f32[128,128]{1,0:T(8,128)S(1)} %get-tuple-element.25.links, ...), custom_call_target="tpu_custom_call" | custom-call | tf_op jit(solution)/shard_map/mix_and_react/pallas_call | solution.py:345
  63.2 0.0 all-to-all-done.1
  63.2 0.6 maximum_bitcast_fusion
  (1 shorter events, 0.0 us)
Async XLA Ops:
  1.9 4.8 %collective-permute-start.2 = (f32[32,128]{1,0:T(8,128)S(1)}, f32[32,128]{1,0:T(8,128)S(1)}, u32[]{:S(2)}, u32[]{:S(2)}) collective-permute-start(f32[32,128]{1,0:T(8,128)S(1)} %get-tuple-element.16), channel_id=1, source_target_pairs={{0,1},{2,3},{4,5},{6,7},{8,9},{10,11},{12,13},{14,15},{16,17},{18,... | collective-permute-start | bytes 49160 | tf_op jit(solution)/shard_map/ppermute | solution.py:304
  3.8 5.1 %collective-permute-start.3 = (f32[32,128]{1,0:T(8,128)S(1)}, f32[32,128]{1,0:T(8,128)S(1)}, u32[]{:S(2)}, u32[]{:S(2)}) collective-permute-start(f32[32,128]{1,0:T(8,128)S(1)} %get-tuple-element.17), channel_id=1, source_target_pairs={{1,2},{3,4},{5,6},{7,8},{9,10},{11,12},{13,14},{15,16},{17,18},{19... | collective-permute-start | bytes 49160 | tf_op jit(solution)/shard_map/ppermute | solution.py:304
  9.5 35.0 %all-to-all-start = ((f32[16,3,4,128]{3,2,1,0:T(4,128)}), f32[16,3,4,128]{3,2,1,0:T(4,128)S(1)}, u32[]{:S(2)}, u32[]{:S(2)}) async-start(f32[16,3,4,128]{3,2,1,0:T(4,128)} %bitcast.15), calls=%async_computation | async-start | bytes 196608 | tf_op jit(solution)/shard_map/all_to_all | solution.py:297
  30.4 14.1 %collective-permute-start.1 = (f32[608,128]{1,0:T(8,128)S(1)}, f32[608,128]{1,0:T(8,128)S(1)}, u32[]{:S(2)}, u32[]{:S(2)}) collective-permute-start(f32[608,128]{1,0:T(8,128)S(1)} %get-tuple-element.15.conc), channel_id=1, source_target_pairs={{64,0},{128,64},{192,128},{256,192},{320,256},{384,320},{448,384},... | collective-permute-start | bytes 933896 | tf_op jit(solution)/shard_map/ppermute | solution.py:287
  31.7 12.8 %collective-permute-start = (f32[608,128]{1,0:T(8,128)S(1)}, f32[608,128]{1,0:T(8,128)S(1)}, u32[]{:S(2)}, u32[]{:S(2)}) collective-permute-start(f32[608,128]{1,0:T(8,128)S(1)} %get-tuple-element.15.conc), channel_id=1, source_target_pairs={{0,64},{64,128},{128,192},{192,256},{256,320},{320,384},{384,448},... | collective-permute-start | bytes 933896 | tf_op jit(solution)/shard_map/ppermute | solution.py:284
  46.9 16.3 %all-to-all-start.1 = ((f32[16,2,128]{2,1,0:T(2,128)}), f32[16,2,128]{2,1,0:T(2,128)S(1)}, u32[]{:S(2)}, u32[]{:S(2)}) async-start(f32[16,2,128]{2,1,0:T(2,128)} %bitcast.9), calls=%async_computation.1 | async-start | bytes 32768 | tf_op jit(solution)/shard_map/all_to_all | solution.py:297

commit v3 on v2

--- a/solution.py
+++ b/solution.py
@@ -33,8 +33,8 @@
 
 
 def minmod(first, second):
-    return jnp.maximum(jnp.minimum(first, second), 0.0) + jnp.minimum(
-        jnp.maximum(first, second), 0.0
+    return jnp.maximum(
+        jnp.minimum(first, second), jnp.minimum(jnp.maximum(first, second), 0.0)
     )
 
 
@@ -114,8 +114,43 @@
     )
 
 
+def second(packed):
+    return pltpu.roll(packed, LANES - 1, 1)
+
+
+def to_ends(packed, place):
+    turn = (LANES - place - 1) % LANES
+    return pltpu.roll(packed, turn, 1) if turn else packed
+
+
+def limit_slopes(
+    conc, below, above, near_got, far_got, own_first, x_slopes, following, slopes, slopes_next
+):
+    lane = lane_index()
+    at_last, at_first = (lane == LANES - 1, lane == 0)
+    left = from_left(near_got, far_got, slice(0, LEV))
+    right = from_right(near_got, far_got, slice(0, LEV))
+    patch = jnp.where(lane % 2 == 1, pltpu.roll(right, 1, 1), own_first[...] - second(left))
+    for t in range(NTR):
+        halves = [slice(t * BLOCK + i * LEV, t * BLOCK + (i + 1) * LEV) for i in range(2)]
+        line = [source[half, :] for source in (below, conc, above) for half in halves]
+        steps = [line[n + 1] - line[n] for n in range(5)]
+        for n in range(4):
+            x_slopes[(4 * t + n) * LEV : (4 * t + n + 1) * LEV, :] = minmod(steps[n], steps[n + 1])
+        for i in range(2):
+            here = line[2 + i]
+            ends = to_ends(patch, 64 * i + 2 * t)
+            after = pltpu.roll(jnp.where(at_first, ends, here), LANES - 1, 1)
+            step = after - here
+            slope = minmod(pltpu.roll(jnp.where(at_last, ends, step), 1, 1), step)
+            following[halves[i], :] = after
+            slopes[halves[i], :] = slope
+            slopes_next[halves[i], :] = pltpu.roll(slope, LANES - 1, 1)
+
+
 def advect_and_heat(
-    chem, conc, below, above, near_got, far_got, own_first, own_last, fields, wet,
+    chem, conc, below, above, x_slopes, following, slopes, slopes_next,
+    near_got, far_got, own_first, own_last, fields, wet,
     moved, heat, ratios, inverses, links, rate, couple, source, answer,
 ):
     lane = lane_index()
@@ -139,78 +174,70 @@
     for i in range(2):
         y_faces.append(face(field(NORTH + i) * wet_f[i] * pltpu.roll(wet_f[i], LANES - 1, 1)))
 
-    def second(packed):
-        return pltpu.roll(packed, LANES - 1, 1)
-
     def edge_flux(courant, lower, upper):
         far_low, near_low = (lower, second(lower))
         near_high, far_high = (upper, second(upper))
         step_low, step, step_high = (near_low - far_low, near_high - near_low, far_high - near_high)
         open_face = ((near_low > 0) & (near_high > 0)).astype(jnp.float32)
-        return (
-            flux(
-                face(courant * open_face), near_low, near_high,
-                minmod(step_low, step), minmod(step, step_high),
-            ),
-            step,
+        return flux(
+            face(courant * open_face), near_low, near_high,
+            minmod(step_low, step), minmod(step, step_high),
         )
 
-    flux_first, step_first = edge_flux(field(EDGE_LOW), left, own_first[...])
-    flux_last, _ = edge_flux(field(EDGE_HIGH), own_last[...], right)
-    odd_lane = lane % 2 == 1
-    patch_steps = jnp.where(odd_lane, pltpu.roll(right, 1, 1), step_first)
-    patch_flux = jnp.where(odd_lane, pltpu.roll(flux_first, 1, 1), flux_last)
-
-    mixture = [jnp.zeros((LEV, LANES), jnp.float32) for _ in range(2)]
-    for t in range(NTR):
-        base = t * BLOCK
-        far_low, near_low = (below[base : base + LEV, :], below[base + LEV : base + BLOCK, :])
-        cells = [conc[base : base + LEV, :], conc[base + LEV : base + BLOCK, :]]
-        near_high, far_high = (above[base : base + LEV, :], above[base + LEV : base + BLOCK, :])
-        line = [far_low, near_low, cells[0], cells[1], near_high, far_high]
-        steps = [line[n + 1] - line[n] for n in range(5)]
-        slopes = [minmod(steps[n], steps[n + 1]) for n in range(4)]
-        x_flux = [
-            flux(x_faces[n], line[n + 1], line[n + 2], slopes[n], slopes[n + 1]) for n in range(3)
-        ]
-        weight = chem[0, t]
-        for i in range(2):
-            here = cells[i]
-            turn = (LANES - (64 * i + 2 * t) - 1) % LANES
-            steps_patch = pltpu.roll(patch_steps, turn, 1) if turn else patch_steps
-            flux_patch = pltpu.roll(patch_flux, turn, 1) if turn else patch_flux
-            following = pltpu.roll(jnp.where(at_first, steps_patch, here), LANES - 1, 1)
-            step = following - here
-            step_before = pltpu.roll(jnp.where(at_last, steps_patch, step), 1, 1)
-            slope = minmod(step_before, step)
-            upper = flux(y_faces[i], here, following, slope, pltpu.roll(slope, LANES - 1, 1))
-            upper = jnp.where(at_last, flux_patch, upper)
-            lower = jnp.where(at_first, flux_patch, pltpu.roll(upper, 1, 1))
-            value = here + (x_flux[i] - x_flux[i + 1]) + (lower - upper)
-            moved[base + i * LEV : base + (i + 1) * LEV, :] = value
-            mixture[i] = mixture[i] + weight * value
+    flux_first = edge_flux(field(EDGE_LOW), left, own_first[...])
+    flux_last = edge_flux(field(EDGE_HIGH), own_last[...], right)
+    patch = jnp.where(lane % 2 == 1, pltpu.roll(flux_first, 1, 1), flux_last)
 
     for i in range(2):
         next_wet = jnp.where(level == LEV - 1, 0.0, pltpu.roll(wet_f[i], LEV - 1, 0))
         coupling = field(KAPPA + i) * wet_f[i] * next_wet
         for r in range(i, 8, 2):
             couple[pl.ds(r, LEV, stride=8), :] = coupling
-            source[pl.ds(r, LEV, stride=8), :] = (
-                moved[i * LEV : (i + 1) * LEV, :] if r < 2 else mixture[i]
-            )
     zero = jnp.zeros((8, LANES), jnp.float32)
-    upper_link, ratio, carried = (zero, zero, zero)
+    upper_link, ratio = (zero, zero)
     for k in range(LEV):
         at = slice(8 * k, 8 * k + 8)
         coupling = couple[at, :]
         inverse = 1.0 / (1.0 + upper_link + coupling + upper_link * ratio)
         ratio = -coupling * inverse
-        carried = (source[at, :] + upper_link * carried) * inverse
         ratios[at, :] = ratio
         inverses[at, :] = inverse
         links[at, :] = upper_link * inverse
+        upper_link = coupling
+
+    mixture = [jnp.zeros((LEV, LANES), jnp.float32) for _ in range(2)]
+    for t in range(NTR):
+        base = t * BLOCK
+        halves = [slice(base + i * LEV, base + (i + 1) * LEV) for i in range(2)]
+        line = [below[halves[1], :], conc[halves[0], :], conc[halves[1], :], above[halves[0], :]]
+        x_slope = [x_slopes[(4 * t + n) * LEV : (4 * t + n + 1) * LEV, :] for n in range(4)]
+        x_flux = [
+            flux(x_faces[n], line[n], line[n + 1], x_slope[n], x_slope[n + 1]) for n in range(3)
+        ]
+        weight = chem[0:1, t : t + 1]
+        for i in range(2):
+            here = line[1 + i]
+            half = halves[i]
+            ends = to_ends(patch, 64 * i + 2 * t)
+            upper = flux(
+                y_faces[i], here, following[half, :], slopes[half, :], slopes_next[half, :]
+            )
+            upper = jnp.where(at_last, ends, upper)
+            lower = jnp.where(at_first, ends, pltpu.roll(upper, 1, 1))
+            value = here + (x_flux[i] - x_flux[i + 1]) + (lower - upper)
+            moved[half, :] = value
+            mixture[i] = mixture[i] + weight * value
+
+    for i in range(2):
+        for r in range(i, 8, 2):
+            source[pl.ds(r, LEV, stride=8), :] = (
+                moved[i * LEV : (i + 1) * LEV, :] if r < 2 else mixture[i]
+            )
+    carried = zero
+    for k in range(LEV):
+        at = slice(8 * k, 8 * k + 8)
+        carried = source[at, :] * inverses[at, :] + links[at, :] * carried
         answer[at, :] = carried
-        upper_link = coupling
     solved = zero
     for k in reversed(range(LEV)):
         at = slice(8 * k, 8 * k + 8)
@@ -231,33 +258,33 @@
 
 
 def mix_and_react(chem, moved, ratios, inverses, links, rate, wet, out, work):
-    shape = (NTR, LANES)
-    for i in range(2):
-        carried = jnp.zeros(shape, jnp.float32)
-        for k in range(LEV):
-            row = slice(8 * k + i, 8 * k + i + 1)
-            at = pl.ds(i * LEV + k, NTR, stride=BLOCK)
-            carried = moved[at, :] * inverses[row, :] + links[row, :] * carried
-            work[at, :] = carried
-        solved = jnp.zeros(shape, jnp.float32)
-        for k in reversed(range(LEV)):
-            row = slice(8 * k + i, 8 * k + i + 1)
-            at = pl.ds(i * LEV + k, NTR, stride=BLOCK)
-            solved = work[at, :] - ratios[row, :] * solved
-            work[at, :] = solved
-    for i in range(2):
-        for half in range(2):
-            start = i * LEV + 8 * half
-            values = [work[t * BLOCK + start : t * BLOCK + start + 8, :] for t in range(NTR)]
-            speed = rate[start : start + 8, :]
-            is_wet = wet[start : start + 8, :]
-            for t in range(NTR):
-                total = chem[t, 0] * values[0]
-                for j in range(1, NTR):
-                    total = total + chem[t, j] * values[j]
-                out[pl.ds(t * BLOCK + 16 * half + i, 8, stride=2), :] = is_wet * (
-                    values[t] + speed * total
-                )
+    pair = range(2)
+    matrix = chem[...]
+
+    def row(k, i):
+        return slice(8 * k + i, 8 * k + i + 1)
+
+    def place(k, i):
+        return slice((2 * k + i) * BLOCK, (2 * k + i) * BLOCK + NTR)
+
+    carried = [jnp.zeros((NTR, LANES), jnp.float32) for i in pair]
+    for k in range(LEV):
+        for i in pair:
+            value = moved[pl.ds(i * LEV + k, NTR, stride=BLOCK), :]
+            carried[i] = value * inverses[row(k, i), :] + links[row(k, i), :] * carried[i]
+            work[place(k, i), :] = carried[i]
+    solved = [jnp.zeros((NTR, LANES), jnp.float32) for i in pair]
+    for k in reversed(range(LEV)):
+        for i in pair:
+            solved[i] = work[place(k, i), :] - ratios[row(k, i), :] * solved[i]
+        reacted = jnp.dot(
+            matrix, jnp.concatenate(solved, axis=1), precision=lax.Precision.HIGHEST,
+            preferred_element_type=jnp.float32,
+        )
+        for i in pair:
+            at = slice(i * LEV + k, i * LEV + k + 1)
+            change = rate[at, :] * reacted[:, i * LANES : (i + 1) * LANES]
+            out[pl.ds(2 * k + i, NTR, stride=BLOCK), :] = wet[at, :] * (solved[i] + change)
 
 
 def shape_of(count):
@@ -277,7 +304,6 @@
     sects = lax.axis_size("sect")
     across = ("tx", "ty")
     strips = lax.axis_size(across)
-    smem = pl.BlockSpec(memory_space=pltpu.SMEM)
     vmem = pl.BlockSpec(memory_space=pltpu.VMEM)
 
     def upward(array, axis, count):
@@ -303,6 +329,7 @@
         pairs = [(n, n + 1) for n in range(start, strips - 1, 2)]
         return lax.ppermute(array, across, pairs + [(high, low) for low, high in pairs])
 
+    limits = pltpu.CompilerParams(vmem_limit_bytes=8 << 20)
     tile, half = (shape_of(NTR * BLOCK), shape_of(LEV))
     conc, sent, near_swap, far_swap, first, last, wet = pl.pallas_call(
         prepare,
@@ -323,20 +350,30 @@
     sent = pl.pallas_call(
         add_left_edge,
         out_shape=jax.ShapeDtypeStruct((LEV * ROWS, LANES), jnp.float32),
+        compiler_params=limits,
         name="add_left_edge",
     )(*near(sent, near_got, far_got))
     fields = exchange(sent.reshape(LEV, ROWS // 4, 4, LANES), FIELD_ROOT)
     fields = flat(fields)
+    limited = pl.pallas_call(
+        limit_slopes,
+        out_shape=(shape_of(NTR * 4 * LEV), tile, tile, tile),
+        compiler_params=limits,
+        name="limit_slopes",
+    )(*near(conc, below, above, near_got, far_got, first))
     column = shape_of(8 * LEV)
     moved, heat, ratios, inverses, links, rate = pl.pallas_call(
         advect_and_heat,
         out_shape=(tile, shape_of(BLOCK), column, column, column, shape_of(BLOCK)),
-        in_specs=[smem] + [vmem] * 9,
+        in_specs=[vmem] * 14,
         scratch_shapes=[pltpu.VMEM((8 * LEV, LANES), jnp.float32)] * 3,
+        compiler_params=limits,
         name="advect_and_heat",
     )(
-        chemistry_matrix,
-        *near(conc, below, above, near_got, far_got, first, last, fields, wet),
+        *near(
+            chemistry_matrix, conc, below, above, *limited, near_got, far_got, first, last,
+            fields, wet,
+        ),
     )
     heating = flat(exchange(heat.reshape(LEV, 2, LANES), HEAT_ROOT))
     turn = 2 * HEAT_ROOT % BLOCK
@@ -345,10 +382,11 @@
     advanced = pl.pallas_call(
         mix_and_react,
         out_shape=jax.ShapeDtypeStruct((NTR * BLOCK, LANES), jnp.float32),
-        in_specs=[smem] + [vmem] * 6,
-        scratch_shapes=[pltpu.VMEM((NTR * BLOCK, LANES), jnp.float32)],
+        in_specs=[vmem] * 7,
+        scratch_shapes=[pltpu.VMEM((BLOCK * BLOCK, LANES), jnp.float32)],
+        compiler_params=limits,
         name="mix_and_react",
-    )(chemistry_matrix, *near(moved, ratios, inverses, links, rate, wet))
+    )(*near(chemistry_matrix, moved, ratios, inverses, links, rate, wet))
     return (
         advanced.reshape(solute_amounts.shape),
         heating.reshape(zonal_boundary_transport.shape),

time: 64.4 us -> 63.9 us (level)
  the two profiles are of different devices: /device:TPU:6 before, /device:TPU:46 now
where the time goes in v3:
time: 63.9 us; the launch traced here: 63.4 us
  starting transfers between devices  44.8 us (70%)
  waiting for transfers between devices  11.6 us (18%)
  Pallas kernels  5.03 us (8%)
  between operations  0.7 us (1%)
  local copies, waits for them, and re-layouts  0.69 us (1%)
    all_to_all x2, starting transfers between devices, exchange(): lax.all_to_all(array, 'sect', split_axis=0, concat_axis=0, tiled=True, ax...  34.2 us
    ppermute x1, waiting for transfers between devices, downward(): return lax.ppermute(array, axis, [(n + 1, n) for n in range(count - 1)])  8.23 us
    ppermute x2, starting transfers between devices, swap(): lax.ppermute(array, across, pairs + [(high, low) for low, high in pairs])  4.76 us
    ppermute x1, starting transfers between devices, upward(): return lax.ppermute(array, axis, [(n, n + 1) for n in range(count - 1)])  4.57 us
    ppermute x2, waiting for transfers between devices, swap(): lax.ppermute(array, across, pairs + [(high, low) for low, high in pairs])  2.2 us
    pallas_call x1, Pallas kernels, body(): pl.pallas_call(mix_and_react, out_shape=jax.ShapeDtypeStruct((NTR * BLOCK...  1.51 us
    ppermute x1, starting transfers between devices, downward(): return lax.ppermute(array, axis, [(n + 1, n) for n in range(count - 1)])  1.28 us
  transfers between devices with their start and end apart: 6, of which 3 were waited for; matrix products, arithmetic and copies ran while one was open for 0% of the time, Pallas kernels for 3%

profile of v3, /device:TPU:46, one launch (start us, length us, event | category | flops | bytes accessed | tf_op | source)
XLA Modules:
  0.0 63.4 jit_solution(10373465208280726527)
XLA Ops:
  0.6 1.3 %prepare.1 = (f32[608,128]{1,0:T(8,128)S(1)}, f32[192,128]{1,0:T(8,128)S(1)}, f32[32,128]{1,0:T(8,128)S(1)}, f32[32,128]{1,0:T(8,128)S(1)}, f32[16,128]{1,0:T(8,...) custom-call(f32[608,128]{1,0:T(8,128)} %bitcast.15, s32[2,128]{1,0:T(2,128)} %tally.1, f32[32,128]{1,0:T(8,128)} %bitcast.19, ...), custom_call_target="tpu_custom_call" | custom-call | tf_op jit(solution)/shard_map/prepare/pallas_call | solution.py:334
  1.9 1.9 %collective-permute-start.2 = (f32[32,128]{1,0:T(8,128)S(1)}, f32[32,128]{1,0:T(8,128)S(1)}, u32[]{:S(2)}, u32[]{:S(2)}) collective-permute-start(f32[32,128]{1,0:T(8,128)S(1)} %get-tuple-element.20), channel_id=1, source_target_pairs={{0,1},{2,3},{4,5},{6,7},{8,9},{10,11},{12,13},{14,15},{16,17},{18,... | collective-permute-start | bytes 49160 | tf_op jit(solution)/shard_map/ppermute | solution.py:330
  3.8 2.8 %collective-permute-start.3 = (f32[32,128]{1,0:T(8,128)S(1)}, f32[32,128]{1,0:T(8,128)S(1)}, u32[]{:S(2)}, u32[]{:S(2)}) collective-permute-start(f32[32,128]{1,0:T(8,128)S(1)} %get-tuple-element.21), channel_id=1, source_target_pairs={{1,2},{3,4},{5,6},{7,8},{9,10},{11,12},{13,14},{15,16},{17,18},{19... | collective-permute-start | bytes 49160 | tf_op jit(solution)/shard_map/ppermute | solution.py:330
  6.7 0.0 collective-permute-done.2.near_got
  6.7 2.2 %collective-permute-done.3.far_got = f32[32,128]{1,0:T(8,128)S(1)} collective-permute-done((f32[32,128]{1,0:T(8,128)S(1)}, f32[32,128]{1,0:T(8,128)S(1)}, u32[]{:S(2)}, u32[]{:S(2)}) %collective-permute-start.3) | collective-permute-done | bytes 16416 | tf_op jit(solution)/shard_map/ppermute | solution.py:330
  8.9 0.7 %add_left_edge.1 = f32[192,128]{1,0:T(8,128)} custom-call(f32[192,128]{1,0:T(8,128)S(1)} %get-tuple-element.28.sent, f32[32,128]{1,0:T(8,128)S(1)} %collective-permute-done.2.near_got, f32[32,128]{1,0:T(8,128)S(1)} %collective-permute-done.3.far_got), custom_call_target="tpu_custom_call" | custom-call | tf_op jit(solution)/shard_map/add_left_edge/pallas_call | solution.py:350
  9.5 20.9 %all-to-all-start = ((f32[16,3,4,128]{3,2,1,0:T(4,128)}), f32[16,3,4,128]{3,2,1,0:T(4,128)S(1)}, u32[]{:S(2)}, u32[]{:S(2)}) async-start(f32[16,3,4,128]{3,2,1,0:T(4,128)} %bitcast.6), calls=%async_computation | async-start | bytes 196608 | tf_op jit(solution)/shard_map/all_to_all | solution.py:323
  30.4 1.3 %collective-permute-start.1 = (f32[608,128]{1,0:T(8,128)S(1)}, f32[608,128]{1,0:T(8,128)S(1)}, u32[]{:S(2)}, u32[]{:S(2)}) collective-permute-start(f32[608,128]{1,0:T(8,128)S(1)} %get-tuple-element.19.conc), channel_id=1, source_target_pairs={{64,0},{128,64},{192,128},{256,192},{320,256},{384,320},{448,384},... | collective-permute-start | bytes 933896 | tf_op jit(solution)/shard_map/ppermute | solution.py:313
  31.7 4.6 %collective-permute-start = (f32[608,128]{1,0:T(8,128)S(1)}, f32[608,128]{1,0:T(8,128)S(1)}, u32[]{:S(2)}, u32[]{:S(2)}) collective-permute-start(f32[608,128]{1,0:T(8,128)S(1)} %get-tuple-element.19.conc), channel_id=1, source_target_pairs={{0,64},{64,128},{128,192},{192,256},{256,320},{320,384},{384,448},... | collective-permute-start | bytes 933896 | tf_op jit(solution)/shard_map/ppermute | solution.py:310
  36.3 8.2 %collective-permute-done.1.above = f32[608,128]{1,0:T(8,128)S(1)} collective-permute-done((f32[608,128]{1,0:T(8,128)S(1)}, f32[608,128]{1,0:T(8,128)S(1)}, u32[]{:S(2)}, u32[]{:S(2)}) %collective-permute-start.1) | collective-permute-done | bytes 311328 | tf_op jit(solution)/shard_map/ppermute | solution.py:313
  44.5 0.0 collective-permute-done.below
  44.5 0.5 limit_slopes.1
  45.0 0.0 copy-start
  45.0 0.0 all-to-all-done
  45.0 0.7 %copy-done = f32[19,19]{1,0:T(8,128)S(1)} copy-done((f32[19,19]{1,0:T(8,128)S(1)}, f32[19,19]{1,0:T(8,128)}, u32[]{:S(2)}) %copy-start) | copy-done | bytes 1468
  45.7 1.1 %advect_and_heat.1 = (f32[608,128]{1,0:T(8,128)S(1)}, f32[32,128]{1,0:T(8,128)}, f32[128,128]{1,0:T(8,128)S(1)}, f32[128,128]{1,0:T(8,128)S(1)}, f32[128,128]{1,0:T(8,128)S(1)}, /*index=5*/f32[32,128]{1,0:T(8,128)S(1)}) custom-call(f32[19,19]{1,0:T(8,128)S(1)} %copy-done, f32[608,128]{1,0:T(8,128)S(1)} %get-tuple-element.19.conc, ...), custom_call_target="tpu_custom_call" | custom-call | tf_op jit(solution)/shard_map/advect_and_heat/pallas_call | solution.py:365
  46.8 13.3 %all-to-all-start.1 = ((f32[16,2,128]{2,1,0:T(2,128)}), f32[16,2,128]{2,1,0:T(2,128)S(1)}, u32[]{:S(2)}, u32[]{:S(2)}) async-start(f32[16,2,128]{2,1,0:T(2,128)} %bitcast.9), calls=%async_computation.1 | async-start | bytes 32768 | tf_op jit(solution)/shard_map/all_to_all | solution.py:323
  60.2 1.5 %mix_and_react.1 = f32[608,128]{1,0:T(8,128)} custom-call(f32[19,19]{1,0:T(8,128)S(1)} %copy-done, f32[608,128]{1,0:T(8,128)S(1)} %get-tuple-element.30.moved, f32[128,128]{1,0:T(8,128)S(1)} %get-tuple-element.31.ratios, f32[128,128]{1,0:T(8,128)S(1)} %get-tuple-element.32.inverses, f32[128,128]{1,0:T(8,128)S(1)} %get-tuple-element.33.links, ...), custom_call_target="tpu_custom_call" | custom-call | tf_op jit(solution)/shard_map/mix_and_react/pallas_call | solution.py:382
  61.7 1.1 %all-to-all-done.1 = f32[16,2,128]{2,1,0:T(2,128)S(1)} async-done(((f32[16,2,128]{2,1,0:T(2,128)}), f32[16,2,128]{2,1,0:T(2,128)S(1)}, u32[]{:S(2)}, u32[]{:S(2)}) %all-to-all-start.1) | async-done | bytes 16416 | tf_op jit(solution)/shard_map/all_to_all | solution.py:323
  62.8 0.6 maximum_bitcast_fusion
  (1 shorter events, 0.0 us)
Async XLA Ops:
  1.9 4.8 %collective-permute-start.2 = (f32[32,128]{1,0:T(8,128)S(1)}, f32[32,128]{1,0:T(8,128)S(1)}, u32[]{:S(2)}, u32[]{:S(2)}) collective-permute-start(f32[32,128]{1,0:T(8,128)S(1)} %get-tuple-element.20), channel_id=1, source_target_pairs={{0,1},{2,3},{4,5},{6,7},{8,9},{10,11},{12,13},{14,15},{16,17},{18,... | collective-permute-start | bytes 49160 | tf_op jit(solution)/shard_map/ppermute | solution.py:330
  3.8 5.1 %collective-permute-start.3 = (f32[32,128]{1,0:T(8,128)S(1)}, f32[32,128]{1,0:T(8,128)S(1)}, u32[]{:S(2)}, u32[]{:S(2)}) collective-permute-start(f32[32,128]{1,0:T(8,128)S(1)} %get-tuple-element.21), channel_id=1, source_target_pairs={{1,2},{3,4},{5,6},{7,8},{9,10},{11,12},{13,14},{15,16},{17,18},{19... | collective-permute-start | bytes 49160 | tf_op jit(solution)/shard_map/ppermute | solution.py:330
  9.5 35.4 %all-to-all-start = ((f32[16,3,4,128]{3,2,1,0:T(4,128)}), f32[16,3,4,128]{3,2,1,0:T(4,128)S(1)}, u32[]{:S(2)}, u32[]{:S(2)}) async-start(f32[16,3,4,128]{3,2,1,0:T(4,128)} %bitcast.6), calls=%async_computation | async-start | bytes 196608 | tf_op jit(solution)/shard_map/all_to_all | solution.py:323
  30.4 14.1 %collective-permute-start.1 = (f32[608,128]{1,0:T(8,128)S(1)}, f32[608,128]{1,0:T(8,128)S(1)}, u32[]{:S(2)}, u32[]{:S(2)}) collective-permute-start(f32[608,128]{1,0:T(8,128)S(1)} %get-tuple-element.19.conc), channel_id=1, source_target_pairs={{64,0},{128,64},{192,128},{256,192},{320,256},{384,320},{448,384},... | collective-permute-start | bytes 933896 | tf_op jit(solution)/shard_map/ppermute | solution.py:313
  31.7 12.8 %collective-permute-start = (f32[608,128]{1,0:T(8,128)S(1)}, f32[608,128]{1,0:T(8,128)S(1)}, u32[]{:S(2)}, u32[]{:S(2)}) collective-permute-start(f32[608,128]{1,0:T(8,128)S(1)} %get-tuple-element.19.conc), channel_id=1, source_target_pairs={{0,64},{64,128},{128,192},{192,256},{256,320},{320,384},{384,448},... | collective-permute-start | bytes 933896 | tf_op jit(solution)/shard_map/ppermute | solution.py:310
  45.0 0.7 %copy-start = (f32[19,19]{1,0:T(8,128)S(1)}, f32[19,19]{1,0:T(8,128)}, u32[]{:S(2)}) copy-start(f32[19,19]{1,0:T(8,128)} %chem.3) | copy-start | bytes 4336
  46.8 16.0 %all-to-all-start.1 = ((f32[16,2,128]{2,1,0:T(2,128)}), f32[16,2,128]{2,1,0:T(2,128)S(1)}, u32[]{:S(2)}, u32[]{:S(2)}) async-start(f32[16,2,128]{2,1,0:T(2,128)} %bitcast.9), calls=%async_computation.1 | async-start | bytes 32768 | tf_op jit(solution)/shard_map/all_to_all | solution.py:323

commit v4 on v3

--- a/solution.py
+++ b/solution.py
@@ -10,9 +10,9 @@
 LEV = 16
 LANES = 128
 BLOCK = 2 * LEV
-ROWS = 12
-EAST_LOW, EAST, NORTH, EDGE_LOW, EDGE_HIGH, KAPPA, GROWTH = 0, 1, 3, 5, 6, 7, 9
-FIELD_ROOT = 12
+ROWS = 10
+EAST_LOW, EAST, NORTH, EDGE_LOW, KAPPA, GROWTH = 0, 1, 3, 5, 6, 8
+FIELD_ROOT = 11
 HEAT_ROOT = 8
 
 
@@ -36,6 +36,11 @@
     return jnp.maximum(
         jnp.minimum(first, second), jnp.minimum(jnp.maximum(first, second), 0.0)
     )
+
+
+def last_columns(pair):
+    ends = [value[:, LANES - 1 :] for value in pair]
+    return jnp.where(lane_index() < LANES // 2, ends[0], ends[1])
 
 
 def prepare(
@@ -50,11 +55,8 @@
     put(EAST_LOW, jnp.where(level == 0, 0.0, pltpu.roll(odd, 1, 0)))
     put(EAST, even)
     put(EAST + 1, odd)
-    pair = [rows(north, i, 2)[:, LANES - 1 :] for i in range(2)]
-    edge = jnp.where(lane < LANES // 2, pair[0], pair[1])
-    put(EDGE_HIGH, edge)
-    for place in (EDGE_LOW, ROWS - 1):
-        put(place, jnp.zeros((LEV, LANES), jnp.float32))
+    edge = last_columns([rows(north, i, 2) for i in range(2)])
+    put(EDGE_LOW, jnp.zeros((LEV, LANES), jnp.float32))
     for i in range(2):
         put(NORTH + i, rows(north, i, 2))
         put(KAPPA + i, rows(kappa, i, 2))
@@ -185,7 +187,9 @@
         )
 
     flux_first = edge_flux(field(EDGE_LOW), left, own_first[...])
-    flux_last = edge_flux(field(EDGE_HIGH), own_last[...], right)
+    flux_last = edge_flux(
+        last_columns([field(NORTH), field(NORTH + 1)]), own_last[...], right
+    )
     patch = jnp.where(lane % 2 == 1, pltpu.roll(flux_first, 1, 1), flux_last)
 
     for i in range(2):
@@ -353,7 +357,7 @@
         compiler_params=limits,
         name="add_left_edge",
     )(*near(sent, near_got, far_got))
-    fields = exchange(sent.reshape(LEV, ROWS // 4, 4, LANES), FIELD_ROOT)
+    fields = exchange(sent.reshape(LEV, ROWS // 2, 2, LANES), FIELD_ROOT)
     fields = flat(fields)
     limited = pl.pallas_call(
         limit_slopes,

time: 63.9 us -> 61.4 us (0.961)
  the two profiles are of different devices: /device:TPU:46 before, /device:TPU:4 now
where the time goes in v4:
time: 61.4 us; the launch traced here: 61.1 us
  starting transfers between devices  47.3 us (77%)
  waiting for transfers between devices  7.34 us (12%)
  Pallas kernels  5.06 us (8%)
  between operations  0.71 us (1%)
    all_to_all x2, starting transfers between devices, exchange(): lax.all_to_all(array, 'sect', split_axis=0, concat_axis=0, tiled=True, ax...  33.7 us
    ppermute x2, starting transfers between devices, swap(): lax.ppermute(array, across, pairs + [(high, low) for low, high in pairs])  7.37 us
    all_to_all x2, waiting for transfers between devices, exchange(): lax.all_to_all(array, 'sect', split_axis=0, concat_axis=0, tiled=True, ax...  7.33 us
    ppermute x1, starting transfers between devices, upward(): return lax.ppermute(array, axis, [(n, n + 1) for n in range(count - 1)])  4.92 us
    pallas_call x1, Pallas kernels, body(): pl.pallas_call(mix_and_react, out_shape=jax.ShapeDtypeStruct((NTR * BLOCK...  1.51 us
    ppermute x1, starting transfers between devices, downward(): return lax.ppermute(array, axis, [(n + 1, n) for n in range(count - 1)])  1.29 us
    pallas_call x1, Pallas kernels, body(): pl.pallas_call(prepare, out_shape=(tile, shape_of(LEV * ROWS), shape_of(B...  1.26 us
  transfers between devices with their start and end apart: 6, of which 2 were waited for; matrix products, arithmetic and copies ran while one was open for 0% of the time, Pallas kernels for 4%

profile of v4, /device:TPU:4, one launch (start us, length us, event | category | flops | bytes accessed | tf_op | source)
XLA Modules:
  0.0 61.1 jit_solution(10407048456952740241)
XLA Ops:
  0.6 1.3 %prepare.1 = (f32[608,128]{1,0:T(8,128)S(1)}, f32[160,128]{1,0:T(8,128)S(1)}, f32[32,128]{1,0:T(8,128)S(1)}, f32[32,128]{1,0:T(8,128)S(1)}, f32[16,128]{1,0:T(8,...) custom-call(f32[608,128]{1,0:T(8,128)} %bitcast.15, s32[2,128]{1,0:T(2,128)} %tally.1, f32[32,128]{1,0:T(8,128)} %bitcast.19, ...), custom_call_target="tpu_custom_call" | custom-call | tf_op jit(solution)/shard_map/prepare/pallas_call | solution.py:338
  1.9 1.9 %collective-permute-start.2 = (f32[32,128]{1,0:T(8,128)S(1)}, f32[32,128]{1,0:T(8,128)S(1)}, u32[]{:S(2)}, u32[]{:S(2)}) collective-permute-start(f32[32,128]{1,0:T(8,128)S(1)} %get-tuple-element.20), channel_id=1, source_target_pairs={{0,1},{2,3},{4,5},{6,7},{8,9},{10,11},{12,13},{14,15},{16,17},{18,... | collective-permute-start | bytes 49160 | tf_op jit(solution)/shard_map/ppermute | solution.py:334
  3.8 5.5 %collective-permute-start.3 = (f32[32,128]{1,0:T(8,128)S(1)}, f32[32,128]{1,0:T(8,128)S(1)}, u32[]{:S(2)}, u32[]{:S(2)}) collective-permute-start(f32[32,128]{1,0:T(8,128)S(1)} %get-tuple-element.21), channel_id=1, source_target_pairs={{1,2},{3,4},{5,6},{7,8},{9,10},{11,12},{13,14},{15,16},{17,18},{19... | collective-permute-start | bytes 49160 | tf_op jit(solution)/shard_map/ppermute | solution.py:334
  9.3 1.3 %collective-permute-start.1 = (f32[608,128]{1,0:T(8,128)S(1)}, f32[608,128]{1,0:T(8,128)S(1)}, u32[]{:S(2)}, u32[]{:S(2)}) collective-permute-start(f32[608,128]{1,0:T(8,128)S(1)} %get-tuple-element.19.conc), channel_id=1, source_target_pairs={{64,0},{128,64},{192,128},{256,192},{320,256},{384,320},{448,384},... | collective-permute-start | bytes 933896 | tf_op jit(solution)/shard_map/ppermute | solution.py:317
  10.6 4.9 %collective-permute-start = (f32[608,128]{1,0:T(8,128)S(1)}, f32[608,128]{1,0:T(8,128)S(1)}, u32[]{:S(2)}, u32[]{:S(2)}) collective-permute-start(f32[608,128]{1,0:T(8,128)S(1)} %get-tuple-element.19.conc), channel_id=1, source_target_pairs={{0,64},{64,128},{128,192},{192,256},{256,320},{320,384},{384,448},... | collective-permute-start | bytes 933896 | tf_op jit(solution)/shard_map/ppermute | solution.py:314
  15.5 0.0 collective-permute-done.2.near_got
  15.5 0.0 collective-permute-done.3.far_got
  15.5 0.7 %add_left_edge.1 = f32[160,128]{1,0:T(8,128)} custom-call(f32[160,128]{1,0:T(8,128)S(1)} %get-tuple-element.28.sent, f32[32,128]{1,0:T(8,128)S(1)} %collective-permute-done.2.near_got, f32[32,128]{1,0:T(8,128)S(1)} %collective-permute-done.3.far_got), custom_call_target="tpu_custom_call" | custom-call | tf_op jit(solution)/shard_map/add_left_edge/pallas_call | solution.py:354
  16.2 21.7 %all-to-all-start = ((f32[16,5,2,128]{3,2,1,0:T(2,128)}), f32[16,5,2,128]{3,2,1,0:T(2,128)S(1)}, u32[]{:S(2)}, u32[]{:S(2)}) async-start(f32[16,5,2,128]{3,2,1,0:T(2,128)} %bitcast.6), calls=%async_computation | async-start | bytes 163840 | tf_op jit(solution)/shard_map/all_to_all | solution.py:327
  37.9 0.0 collective-permute-done.1.above
  37.9 0.0 collective-permute-done.below
  37.9 0.5 limit_slopes.1
  38.4 0.0 copy-start
  38.4 6.2 %all-to-all-done = f32[16,5,2,128]{3,2,1,0:T(2,128)S(1)} async-done(((f32[16,5,2,128]{3,2,1,0:T(2,128)}), f32[16,5,2,128]{3,2,1,0:T(2,128)S(1)}, u32[]{:S(2)}, u32[]{:S(2)}) %all-to-all-start) | async-done | bytes 81952 | tf_op jit(solution)/shard_map/all_to_all | solution.py:327
  44.6 0.0 copy-done
  44.6 1.2 %advect_and_heat.1 = (f32[608,128]{1,0:T(8,128)S(1)}, f32[32,128]{1,0:T(8,128)}, f32[128,128]{1,0:T(8,128)S(1)}, f32[128,128]{1,0:T(8,128)S(1)}, f32[128,128]{1,0:T(8,128)S(1)}, /*index=5*/f32[32,128]{1,0:T(8,128)S(1)}) custom-call(f32[19,19]{1,0:T(8,128)S(1)} %copy-done, f32[608,128]{1,0:T(8,128)S(1)} %get-tuple-element.19.conc, ...), custom_call_target="tpu_custom_call" | custom-call | tf_op jit(solution)/shard_map/advect_and_heat/pallas_call | solution.py:369
  45.8 12.0 %all-to-all-start.1 = ((f32[16,2,128]{2,1,0:T(2,128)}), f32[16,2,128]{2,1,0:T(2,128)S(1)}, u32[]{:S(2)}, u32[]{:S(2)}) async-start(f32[16,2,128]{2,1,0:T(2,128)} %bitcast.9), calls=%async_computation.1 | async-start | bytes 32768 | tf_op jit(solution)/shard_map/all_to_all | solution.py:327
  57.8 1.5 %mix_and_react.1 = f32[608,128]{1,0:T(8,128)} custom-call(f32[19,19]{1,0:T(8,128)S(1)} %copy-done, f32[608,128]{1,0:T(8,128)S(1)} %get-tuple-element.30.moved, f32[128,128]{1,0:T(8,128)S(1)} %get-tuple-element.31.ratios, f32[128,128]{1,0:T(8,128)S(1)} %get-tuple-element.32.inverses, f32[128,128]{1,0:T(8,128)S(1)} %get-tuple-element.33.links, ...), custom_call_target="tpu_custom_call" | custom-call | tf_op jit(solution)/shard_map/mix_and_react/pallas_call | solution.py:386
  59.3 1.1 %all-to-all-done.1 = f32[16,2,128]{2,1,0:T(2,128)S(1)} async-done(((f32[16,2,128]{2,1,0:T(2,128)}), f32[16,2,128]{2,1,0:T(2,128)S(1)}, u32[]{:S(2)}, u32[]{:S(2)}) %all-to-all-start.1) | async-done | bytes 16416 | tf_op jit(solution)/shard_map/all_to_all | solution.py:327
  60.4 0.6 maximum_bitcast_fusion
  (1 shorter events, 0.0 us)
Async XLA Ops:
  1.9 13.6 %collective-permute-start.2 = (f32[32,128]{1,0:T(8,128)S(1)}, f32[32,128]{1,0:T(8,128)S(1)}, u32[]{:S(2)}, u32[]{:S(2)}) collective-permute-start(f32[32,128]{1,0:T(8,128)S(1)} %get-tuple-element.20), channel_id=1, source_target_pairs={{0,1},{2,3},{4,5},{6,7},{8,9},{10,11},{12,13},{14,15},{16,17},{18,... | collective-permute-start | bytes 49160 | tf_op jit(solution)/shard_map/ppermute | solution.py:334
  3.8 11.7 %collective-permute-start.3 = (f32[32,128]{1,0:T(8,128)S(1)}, f32[32,128]{1,0:T(8,128)S(1)}, u32[]{:S(2)}, u32[]{:S(2)}) collective-permute-start(f32[32,128]{1,0:T(8,128)S(1)} %get-tuple-element.21), channel_id=1, source_target_pairs={{1,2},{3,4},{5,6},{7,8},{9,10},{11,12},{13,14},{15,16},{17,18},{19... | collective-permute-start | bytes 49160 | tf_op jit(solution)/shard_map/ppermute | solution.py:334
  9.3 28.6 %collective-permute-start.1 = (f32[608,128]{1,0:T(8,128)S(1)}, f32[608,128]{1,0:T(8,128)S(1)}, u32[]{:S(2)}, u32[]{:S(2)}) collective-permute-start(f32[608,128]{1,0:T(8,128)S(1)} %get-tuple-element.19.conc), channel_id=1, source_target_pairs={{64,0},{128,64},{192,128},{256,192},{320,256},{384,320},{448,384},... | collective-permute-start | bytes 933896 | tf_op jit(solution)/shard_map/ppermute | solution.py:317
  10.6 27.3 %collective-permute-start = (f32[608,128]{1,0:T(8,128)S(1)}, f32[608,128]{1,0:T(8,128)S(1)}, u32[]{:S(2)}, u32[]{:S(2)}) collective-permute-start(f32[608,128]{1,0:T(8,128)S(1)} %get-tuple-element.19.conc), channel_id=1, source_target_pairs={{0,64},{64,128},{128,192},{192,256},{256,320},{320,384},{384,448},... | collective-permute-start | bytes 933896 | tf_op jit(solution)/shard_map/ppermute | solution.py:314
  16.2 28.4 %all-to-all-start = ((f32[16,5,2,128]{3,2,1,0:T(2,128)}), f32[16,5,2,128]{3,2,1,0:T(2,128)S(1)}, u32[]{:S(2)}, u32[]{:S(2)}) async-start(f32[16,5,2,128]{3,2,1,0:T(2,128)} %bitcast.6), calls=%async_computation | async-start | bytes 163840 | tf_op jit(solution)/shard_map/all_to_all | solution.py:327
  38.4 6.2 %copy-start = (f32[19,19]{1,0:T(8,128)S(1)}, f32[19,19]{1,0:T(8,128)}, u32[]{:S(2)}) copy-start(f32[19,19]{1,0:T(8,128)} %chem.3) | copy-start | bytes 4336
  45.8 14.7 %all-to-all-start.1 = ((f32[16,2,128]{2,1,0:T(2,128)}), f32[16,2,128]{2,1,0:T(2,128)S(1)}, u32[]{:S(2)}, u32[]{:S(2)}) async-start(f32[16,2,128]{2,1,0:T(2,128)} %bitcast.9), calls=%async_computation.1 | async-start | bytes 32768 | tf_op jit(solution)/shard_map/all_to_all | solution.py:327
